TPU v7x, 32 devices: a whole 2x2x4 slice. The times are simulated.
32 devices in a mesh: groups: 2 (over y), frame: 8 (over z, x), head: 2 (over core).
Axes of the slice: x: 2, y: 2, z: 4, core: 2. Of those that a mesh axis runs over, the one named last changes fastest.
Arguments:
- stream: bfloat16 [2048, 2240], P(('groups', 'frame'), 'head'), parts along dimension 0, may hold values from -24 to 24
- queries: bfloat16 [2048, 1120], P(('groups', 'frame'), 'head'), parts along dimension 0, may hold values from -6 to 6
- key_rows: bfloat16 [2048, 1120], P(('groups', 'frame'), 'head'), parts along dimension 0, may hold values from -6 to 6
- value_rows: bfloat16 [2048, 1120], P(('groups', 'frame'), 'head'), parts along dimension 0, may hold values from -16 to 16
- attn_gain: float32 [1120], P('head'), may hold values from 0.25 to 1.75
- w_out: bfloat16 [1120, 2240], P('head', 'frame'), may hold values from -0.1875 to 0.1875
- ffn_gain: float32 [2240], replicated, may hold values from 0.25 to 1.75
- w_up: bfloat16 [2240, 3360], P('frame', 'head'), may hold values from -0.125 to 0.125
- conv_taps: float32 [3, 3360], P(None, 'head'), may hold values from -3 to 3
- w_down: bfloat16 [3360, 2240], P('head', 'frame'), may hold values from -0.109375 to 0.109375
Outputs:
- block_out: bfloat16 [2048, 2240], P(('groups', 'frame'), 'head'), parts along dimension 0
There are 2 independent parts, one for each index of `groups`. A program takes and returns all parts, laid end to end along the dimension named above; an argument that names none is the same for every part. Nothing has to cross between parts.
All inputs are finite; a program needn't handle non-finite values.
Results may differ from a plain program's by a relative error of at most 0.0058.
Values may be sent and summed in bfloat16 or wider, within the bound.
A program may use at most 128 MiB of HBM per device.

v0:
```python
import jax
import jax.numpy as jnp
from jax import lax
from jax.sharding import PartitionSpec as P

D = 2240
HEADS = 10
HEAD_DIM = 112
TPF = 128


def prefix(x, axis, combine, identity):
    length, place = (lax.axis_size(axis), lax.axis_index(axis))
    everything = jax.tree.map(lambda part: lax.all_gather(part, axis), x)
    start = jax.tree.map(
        lambda part, zero: jnp.broadcast_to(jnp.asarray(zero, part.dtype), part.shape), x, identity
    )

    def hop(k, before):
        reached = k < place
        new = combine(before, jax.tree.map(lambda part: part[k], everything))
        return jax.tree.map(lambda a, b: jnp.where(reached, a, b), new, before)

    return lax.fori_loop(0, length, hop, start)


def padded_2(block, sides, width):
    for axis, dim in sides:
        count = lax.axis_size(axis)
        forward = [(i, i + 1) for i in range(count - 1)]
        backward = [(target, source) for source, target in forward]
        low = lax.ppermute(
            lax.slice_in_dim(block, block.shape[dim] - width, None, axis=dim), axis, forward
        )
        high = lax.ppermute(lax.slice_in_dim(block, 0, width, axis=dim), axis, backward)
        block = jnp.concatenate([low, block, high], axis=dim)
    return block


def add_pair(earlier, later):
    return (earlier[0] + later[0], earlier[1] + later[1])


def body(
    stream, queries, key_rows, value_rows, attn_gain, w_out, ffn_gain, w_up, conv_taps, w_down
):
    highest = lax.Precision.HIGHEST
    tokens_here = queries.shape[0]
    frames_here = tokens_here // TPF
    heads_here = queries.shape[1] // HEAD_DIM
    qpos = jnp.maximum(queries.astype(jnp.float32), 0.0).reshape(
        frames_here, TPF, heads_here, HEAD_DIM
    )
    kpos = jnp.maximum(key_rows.astype(jnp.float32), 0.0).reshape(
        frames_here, TPF, heads_here, HEAD_DIM
    )
    values = value_rows.astype(jnp.float32).reshape(frames_here, TPF, heads_here, HEAD_DIM)
    frame_state = jnp.einsum("fthb,fthc->fhbc", kpos, values, precision=highest)
    frame_keys = jnp.sum(kpos, axis=1)
    own_state = jnp.sum(frame_state, axis=0)
    own_keys = jnp.sum(frame_keys, axis=0)
    empty_state = jnp.zeros_like(own_state)
    empty_keys = jnp.zeros_like(own_keys)
    before_state, before_keys = prefix(
        (own_state, own_keys), "frame", add_pair, (empty_state, empty_keys)
    )
    state = before_state[None] + jnp.cumsum(frame_state, axis=0)
    key_total = before_keys[None] + jnp.cumsum(frame_keys, axis=0)
    numer = jnp.einsum("fthb,fhbc->fthc", qpos, state, precision=highest)
    denom = jnp.einsum("fthb,fhb->fth", qpos, key_total, precision=highest) + 1e-06
    attended = (numer / denom[..., None]).reshape(tokens_here, heads_here * HEAD_DIM)
    squares = lax.psum(jnp.sum(attended * attended, axis=1), "head")
    scale = lax.rsqrt(squares / (HEADS * HEAD_DIM) + 1e-06)
    normed = (attended * scale[:, None] * attn_gain).astype(jnp.bfloat16)
    width_here = stream.shape[1]
    first_col = lax.axis_index("head") * width_here
    gain_here = lax.dynamic_slice_in_dim(ffn_gain, first_col, width_here, 0)
    proj = jnp.dot(
        normed,
        lax.all_gather(w_out, "frame", axis=1, tiled=True),
        preferred_element_type=jnp.float32,
    )
    proj_mine = lax.psum_scatter(proj, "head", scatter_dimension=1, tiled=True)
    resid_mine = (stream.astype(jnp.float32) + proj_mine).astype(jnp.bfloat16)
    resid_mine = lax.optimization_barrier(resid_mine)
    resid_float = resid_mine.astype(jnp.float32)
    total_sq = lax.psum(jnp.sum(resid_float * resid_float, axis=1), "head")
    inverse = lax.rsqrt(total_sq / D + 1e-06)
    normed_part = (resid_float * inverse[:, None] * gain_here).astype(jnp.bfloat16)
    ffn_in = lax.all_gather(normed_part, "head", axis=1, tiled=True)
    hidden_here = w_up.shape[1]
    up_value = jnp.dot(
        ffn_in,
        lax.all_gather(w_up, "frame", axis=0, tiled=True),
        preferred_element_type=jnp.float32,
    )
    hidden = (
        jax.nn.silu(up_value).astype(jnp.bfloat16).reshape(ffn_in.shape[0] // TPF, TPF, hidden_here)
    )
    padded = padded_2(hidden, (("frame", 0),), 1)
    padded_float = padded.astype(jnp.float32)
    mixed = (
        conv_taps[0] * padded_float[:-2]
        + conv_taps[1] * padded_float[1:-1]
        + conv_taps[2] * padded_float[2:]
    )
    mixed = mixed.astype(jnp.bfloat16).reshape(tokens_here, hidden_here)
    ffn_terms = jnp.dot(
        mixed,
        lax.all_gather(w_down, "frame", axis=1, tiled=True),
        preferred_element_type=jnp.float32,
    )
    ffn_mine = lax.psum_scatter(ffn_terms, "head", scatter_dimension=1, tiled=True)
    return (resid_float + ffn_mine).astype(jnp.bfloat16)


def solution(mesh):
    in_specs = (
        P(("groups", "frame"), "head"),
        P(("groups", "frame"), "head"),
        P(("groups", "frame"), "head"),
        P(("groups", "frame"), "head"),
        P("head"),
        P("head", "frame"),
        P(),
        P("frame", "head"),
        P(None, "head"),
        P("head", "frame"),
    )
    out_specs = P(("groups", "frame"), "head")
    return jax.shard_map(body, mesh=mesh, in_specs=in_specs, out_specs=out_specs, check_vma=False)
```

profile of v0, /device:TPU:0, one launch (start us, length us, event | category | flops | bytes accessed | tf_op | source)
XLA Modules:
  0.0 408.5 jit_solution(7694637716419283714)
XLA Ops:
  6.5 1.1 fusion.18
  7.6 1.1 fusion.22
  8.8 0.0 all-gather.6.cloned.1.call-start
  8.8 0.7 all-gather.6.cloned.1.call-update
  9.5 0.0 reduce-scatter.3.cloned.1.call-start
  9.6 0.1 reduce_sum.40
  9.7 0.1 reduce_sum.41
  9.8 32.4 %all_gather.21 = f32[8,5,112]{2,1,0:T(8,128)S(1)} all-gather(f32[1,5,112]{2,1,0:T(8,128)S(1)} %reduce_sum.40), channel_id=1, replica_groups=mesh['groups'=2,'frame'=8,'head'=2] {'frame'}, dimensions={0}, use_global_device_ids=true | all-gather | bytes 20160 | tf_op jit(solution)/shard_map/all_gather | solution.py:14
  42.2 1.0 convert_maximum_fusion
  43.2 20.4 %all-gather.12.cloned.1.call-done = f32[40,112,112]{2,1,0:T(8,128)} async-done(((f32[5,112,112]{2,1,0:T(8,128)}), f32[40,112,112]{2,1,0:T(8,128)}) %all-gather.12.cloned.1.call-update) | async-done | bytes 2007056 | tf_op jit(solution)/shard_map/all_gather | solution.py:14
  63.5 8.8 %while.16 = (s32[]{:T(128)}, f32[5,112,112]{2,1,0:T(8,128)S(1)}, f32[5,112]{1,0:T(8,128)S(1)}, s32[]{:T(128)}, f32[8,5,112,112]{3,2,1,0:T(8,128)}, /*index=5*/f32[8,5,112]{2,1,0:T(8,128)S(1)}, s32[]{:T(128)}, s32[]{:T(128)}) while((s32[]{:T(128)}, f32[5,112,112]{2,1,0:T(8,128)S(1)}, f32[5,112]{1,0:T(8,128)S(1)}, s32[]{:T(128)}, ...), condition=%wide.region_2.0_spmd.clone, body=%wide.region_1.0_spmd.clone.sunk | while | flops 189844 | bytes 759475 | solution.py:24
  63.5 1.1 add_select_fusion.4
  64.6 1.0 add_select_fusion.4
  65.7 1.0 add_select_fusion.4
  66.8 1.0 add_select_fusion.4
  67.9 1.0 add_select_fusion.4
  69.0 1.0 add_select_fusion.4
  70.1 1.0 add_select_fusion.4
  71.2 1.1 add_select_fusion.4
  72.3 0.3 fusion.20
  72.7 0.7 multiply_reduce_fusion
  73.3 2.5 psum.14
  75.8 0.1 fusion.16
  76.0 45.3 %all-gather.6.cloned.1.call-done = bf16[560,2240]{0,1:T(8,128)(2,1)} async-done(((bf16[560,280]{0,1:T(8,128)(2,1)}), bf16[560,2240]{0,1:T(8,128)(2,1)}) %all-gather.6.cloned.1.call-update) | async-done | bytes 2508816 | tf_op jit(solution)/shard_map/all_gather | solution.py:80
  121.3 3.7 fusion.23
  125.1 0.0 all-gather.8.cloned.1.call-start
  125.1 0.5 all-gather.8.cloned.1.call-update
  125.7 0.0 all-gather.10.cloned.1.call-start
  125.7 0.5 all-gather.10.cloned.1.call-update
  126.2 0.0 reduce-scatter.5.cloned.1.call-start
  126.3 0.1 dynamic_slice.17
  126.4 5.9 %reduce-scatter.3.cloned.1.call-done = f32[128,1120]{0,1:T(8,128)} async-done(((f32[128,2240]{0,1:T(8,128)}), f32[128,1120]{0,1:T(8,128)}) %reduce-scatter.3.cloned.1.call-update) | async-done | bytes 573456 | tf_op jit(solution)/shard_map/reduce_scatter | solution.py:83
  132.3 1.1 add_convert_fusion
  133.5 0.2 fusion.4
  133.6 2.5 psum.15
  136.1 0.2 fusion.6
  136.3 2.2 all_gather.23
  138.5 117.0 %all-gather.8.cloned.1.call-done = bf16[2240,1680]{1,0:T(8,128)(2,1)} async-done(((bf16[280,1680]{1,0:T(8,128)(2,1)}), bf16[2240,1680]{1,0:T(8,128)(2,1)}) %all-gather.8.cloned.1.call-update) | async-done | bytes 7526416 | tf_op jit(solution)/shard_map/all_gather | solution.py:94
  255.6 6.5 %fusion.14 = bf16[1,128,1680]{1,2,0:T(8,128)(2,1)S(1)} fusion(bf16[128,2240]{0,1:T(8,128)(2,1)S(1)} %all_gather.23, bf16[2240,1680]{1,0:T(8,128)(2,1)} %all-gather.8.cloned.1.call-done), kind=kOutput, calls=%fused_computation.25 | convolution fusion | flops 964454400 | bytes 8529920 | tf_op jit(solution)/shard_map/dot_general | solution.py:92
  262.1 2.5 collective-permute-start
  264.6 1.3 collective-permute-start.1
  265.9 0.1 slice_reduce_fusion.2
  266.0 23.9 %collective-permute-done = bf16[1,128,1680]{1,2,0:T(8,128)(2,1)S(1)} collective-permute-done((bf16[1,128,1680]{1,2,0:T(8,128)(2,1)S(1)}, bf16[1,128,1680]{1,2,0:T(8,128)(2,1)S(1)}, u32[]{:S(2)}, u32[]{:S(2)}) %collective-permute-start) | collective-permute-done | bytes 430112 | tf_op jit(solution)/shard_map/ppermute | solution.py:32
  289.9 0.2 maximum_convert_fusion
  290.1 95.9 %all-gather.10.cloned.1.call-done = bf16[1680,2240]{0,1:T(8,128)(2,1)} async-done(((bf16[1680,280]{0,1:T(8,128)(2,1)}), bf16[1680,2240]{0,1:T(8,128)(2,1)}) %all-gather.10.cloned.1.call-update) | async-done | bytes 7526416 | tf_op jit(solution)/shard_map/all_gather | solution.py:110
  386.0 6.9 %fusion.9 = f32[128,2240]{0,1:T(8,128)} fusion(bf16[1680,2240]{0,1:T(8,128)(2,1)} %all-gather.10.cloned.1.call-done, f32[3,128,1680]{1,2,0:T(8,128)S(1)} %maximum_convert_fusion, f32[1680]{0:T(1024)S(1)} %get-tuple-element.139, f32[1680]{0:T(1024)S(1)} %get-tuple-element.140, f32[1680]{0:T(1024)S(1)} %get-tuple-element.138), kind=kOutput, calls=%fused_computation.21 | convolution fusion | flops 964669440 | bytes 11273920 | tf_op jit(solution)/shard_map/dot_general | solution.py:108
  393.0 6.8 %reduce-scatter.5.cloned.1.call-done = f32[128,1120]{0,1:T(8,128)} async-done(((f32[128,2240]{0,1:T(8,128)}), f32[128,1120]{0,1:T(8,128)}) %reduce-scatter.5.cloned.1.call-update) | async-done | bytes 573456 | tf_op jit(solution)/shard_map/reduce_scatter | solution.py:113
  399.8 1.8 fusion.7
  (31 shorter events, 0.2 us)
Async XLA Ops:
  6.5 1.1 copy-start
  6.5 57.0 %all-gather.12.cloned.1.call-start = ((), (), s32[]{:S(2)}) async-start(), calls=%async_computation.7 | async-start | bytes 2580480 | tf_op jit(solution)/shard_map/all_gather | solution.py:14
  8.8 112.5 %all-gather.6.cloned.1.call-start = ((), (), s32[]{:S(2)}) async-start(), calls=%async_computation.2 | async-start | bytes 3225600 | tf_op jit(solution)/shard_map/all_gather | solution.py:80
  9.5 122.8 %reduce-scatter.3.cloned.1.call-start = ((), (), s32[]{:S(2)}) async-start(), calls=%async_computation.3 | async-start | bytes 1720320 | tf_op jit(solution)/shard_map/reduce_scatter | solution.py:83
  42.2 30.5 %copy-start.1 = (f32[5,112,112]{2,1,0:T(8,128)S(1)}, f32[5,112,112]{2,1,0:T(8,128)}, u32[]{:S(2)}) copy-start(f32[5,112,112]{2,1,0:T(8,128)} %fusion.22) | copy-start | bytes 752644
  63.5 12.3 %copy-start.5 = (f32[560]{0:T(1024)S(1)}, f32[560]{0:T(1024)}, u32[]{:S(2)}) copy-start(f32[560]{0:T(1024)} %param.16) | copy-start | bytes 6724
  125.0 1.2 copy-start.4
  125.0 7.3 %copy-start.2 = (bf16[128,1120]{0,1:T(8,128)(2,1)S(1)}, bf16[128,1120]{0,1:T(8,128)(2,1)}, u32[]{:S(2)}) copy-start(bf16[128,1120]{0,1:T(8,128)(2,1)} %param.12) | copy-start | bytes 860164
  125.1 130.5 %all-gather.8.cloned.1.call-start = ((), (), s32[]{:S(2)}) async-start(), calls=%async_computation.4 | async-start | bytes 9031680 | tf_op jit(solution)/shard_map/all_gather | solution.py:94
  125.7 260.4 %all-gather.10.cloned.1.call-start = ((), (), s32[]{:S(2)}) async-start(), calls=%async_computation.5 | async-start | bytes 9031680 | tf_op jit(solution)/shard_map/all_gather | solution.py:110
  126.2 273.5 %reduce-scatter.5.cloned.1.call-start = ((), (), s32[]{:S(2)}) async-start(), calls=%async_computation.6 | async-start | bytes 1720320 | tf_op jit(solution)/shard_map/reduce_scatter | solution.py:113
  138.5 127.4 %copy-start.3 = (f32[3,1680]{1,0:T(4,128)S(1)}, f32[3,1680]{1,0:T(4,128)}, u32[]{:S(2)}) copy-start(f32[3,1680]{1,0:T(4,128)} %param.20) | copy-start | bytes 60484
  262.1 27.8 %collective-permute-start = (bf16[1,128,1680]{1,2,0:T(8,128)(2,1)S(1)}, bf16[1,128,1680]{1,2,0:T(8,128)(2,1)S(1)}, u32[]{:S(2)}, u32[]{:S(2)}) collective-permute-start(bf16[1,128,1680]{1,2,0:T(8,128)(2,1)S(1)} %fusion.14), channel_id=1, source_target_pairs={{0,2},{2,4},{4,6},{6,8},{8,10},{10,12},{12,14},{1,3},{3,5},{5,7},{... | collective-permute-start | bytes 1290248 | tf_op jit(solution)/shard_map/ppermute | solution.py:32
  264.6 25.3 %collective-permute-start.1 = (bf16[1,128,1680]{1,2,0:T(8,128)(2,1)S(1)}, bf16[1,128,1680]{1,2,0:T(8,128)(2,1)S(1)}, u32[]{:S(2)}, u32[]{:S(2)}) collective-permute-start(bf16[1,128,1680]{1,2,0:T(8,128)(2,1)S(1)} %fusion.14), channel_id=1, source_target_pairs={{2,0},{4,2},{6,4},{8,6},{10,8},{12,10},{14,12},{3,1},{5,3},{7,5},{... | collective-permute-start | bytes 1290248 | tf_op jit(solution)/shard_map/ppermute | solution.py:35
Sparse Core Ops, SparseCore 0:
  9.5 53.9 all-gather.11
  65.7 55.5 all-gather.5
  125.2 7.0 reduce-scatter.2
  134.4 121.1 all-gather.7
  257.6 128.4 all-gather.9
  393.1 6.6 reduce-scatter.4
where the time goes:
time: 409 us; the launch traced here: 408 us
  waiting for transfers between devices  317 us (78%)
  blocking collectives  39.6 us (10%)
  matrix products  19.3 us (5%)
  other arithmetic  14.3 us (3%)
  between operations  13.6 us (3%)
    all_gather x1, waiting for transfers between devices, body(): lax.all_gather(w_up, 'frame', axis=0, tiled=True)  117 us
    all_gather x1, waiting for transfers between devices, body(): lax.all_gather(w_down, 'frame', axis=1, tiled=True)  95.9 us
    all_gather x1, waiting for transfers between devices, body(): lax.all_gather(w_out, 'frame', axis=1, tiled=True)  45.3 us
    all_gather x1, blocking collectives, prefix(): everything = jax.tree.map(lambda part: lax.all_gather(part, axis), x)  32.4 us
    ppermute x1, waiting for transfers between devices, padded_2(): lax.ppermute(lax.slice_in_dim(block, block.shape[dim] - width, None, axis...  23.9 us
    all_gather x1, waiting for transfers between devices, prefix(): everything = jax.tree.map(lambda part: lax.all_gather(part, axis), x)  20.4 us
    select_n x16, other arithmetic, hop(): return jax.tree.map(lambda a, b: jnp.where(reached, a, b), new, before)  8.52 us
  transfers between devices with their start and end apart: 8, of which 7 were waited for; matrix products, arithmetic and copies ran while one was open for 5% of the time, Pallas kernels for 0%

commit v1 on v0

--- a/solution.py
+++ b/solution.py
@@ -1,6 +1,10 @@
+import functools
+
 import jax
 import jax.numpy as jnp
 from jax import lax
+from jax.experimental import pallas as pl
+from jax.experimental.pallas import tpu as pltpu
 from jax.sharding import PartitionSpec as P
 
 D = 2240
@@ -114,6 +118,354 @@
     return (resid_float + ffn_mine).astype(jnp.bfloat16)
 
 
+MESH_ID = pl.DeviceIdType.MESH
+
+
+def ring_frame(pos, n):
+    late = pos // (n // 2)
+    return (1 - late) * (2 * pos) + late * (2 * (n - 1 - pos) + 1)
+
+
+def ring_place(frame, n):
+    odd = frame % 2
+    return (1 - odd) * (frame // 2) + odd * (n - 1 - frame // 2)
+
+
+def greet(partners):
+    barrier = pltpu.get_barrier_semaphore()
+    for partner in partners:
+        pl.semaphore_signal(barrier, inc=1, device_id=partner, device_id_type=MESH_ID)
+    pl.semaphore_wait(barrier, len(partners))
+
+
+def remote(src, dst, send, recv, device):
+    return pltpu.make_async_remote_copy(
+        src_ref=src, dst_ref=dst, send_sem=send, recv_sem=recv,
+        device_id=device, device_id_type=MESH_ID,
+    )
+
+
+def ring_steps(n):
+    far = n // 2
+    return [
+        (step, way, half)
+        for step in range(1, far + 1)
+        for half in range(2)
+        for way in range(2)
+        if step < far or way == half
+    ]
+
+
+def ring_gather(buffer, place, n, send, recv, on_arrival):
+    ends = [ring_frame((place + 1) % n, n), ring_frame((place + n - 1) % n, n)]
+    started = []
+
+    def origin(step, way):
+        back = step if way == 0 else n - step
+        return ring_frame((place + n - back) % n, n)
+
+    def arrive(step, way, half):
+        source = origin(step, way)
+        slot = buffer(source, half)
+        remote(slot, slot, send.at[way, step, half], recv.at[way, step, half],
+               {"frame": ends[way]}).wait_recv()
+        on_arrival(source, half)
+
+    for step, way, half in ring_steps(n):
+        if step > 1:
+            arrive(step - 1, way, half)
+        slot = buffer(origin(step - 1, way), half)
+        copy = remote(slot, slot, send.at[way, step, half], recv.at[way, step, half],
+                      {"frame": ends[way]})
+        copy.start()
+        started.append(copy)
+    for step, way, half in ring_steps(n):
+        last = n // 2 if way == half else n // 2 - 1
+        if step == last:
+            arrive(step, way, half)
+    for copy in started:
+        copy.wait_send()
+
+
+def first_kernel(n, state_ref, up_ref, down_ref, states, up_out, down_out, here,
+                 ring_send, ring_recv, all_send, all_recv):
+    frame = lax.axis_index("frame")
+    place = ring_place(frame, n)
+    local = [
+        pltpu.make_async_copy(state_ref, states.at[frame], here.at[0]),
+        pltpu.make_async_copy(up_ref.at[frame], up_out.at[frame], here.at[1]),
+        pltpu.make_async_copy(down_ref.at[frame], down_out.at[frame], here.at[2]),
+    ]
+    for copy in local:
+        copy.start()
+    greet([{"frame": (frame + k) % n} for k in range(1, n)])
+    local[0].wait()
+    pushes = []
+    for at, (src, dst) in enumerate(((up_ref, up_out), (down_ref, down_out))):
+        for k in range(1, n):
+            target = (frame + k) % n
+            copy = remote(src.at[target], dst.at[frame], all_send.at[at, k],
+                          all_recv.at[at, k], {"frame": target})
+            pushes.append((copy, at, k))
+    for copy, at, k in pushes:
+        copy.start()
+    ring_gather(lambda source, half: states.at[source, half], place, n,
+                ring_send, ring_recv, lambda source, half: None)
+    for copy, at, k in pushes:
+        copy.wait_send()
+        source = (frame + n - k) % n
+        dst = (up_out, down_out)[at]
+        remote(dst.at[source], dst.at[source], all_send.at[at, k], all_recv.at[at, k],
+               {"frame": source}).wait_recv()
+    local[1].wait()
+    local[2].wait()
+
+
+def second_kernel(n, features, width, own_ref, other_ref, sq_ref, stream_ref, gain_ref,
+                  everything, resid, arrived, sq_in, sq_mine, sq_two,
+                  pair_send, pair_recv, ring_send, ring_recv, twin_send, twin_recv):
+    frame, head = lax.axis_index("frame"), lax.axis_index("head")
+    place = ring_place(frame, n)
+    twin = {"head": 1 - head}
+    greet([twin, {"frame": ring_frame((place + 1) % n, n)},
+           {"frame": ring_frame((place + n - 1) % n, n)}])
+    first = remote(other_ref, arrived, pair_send.at[0], pair_recv.at[0], twin)
+    second = remote(sq_ref, sq_in, pair_send.at[1], pair_recv.at[1], twin)
+    second.start()
+    first.start()
+    second.wait()
+    scale = lax.rsqrt((sq_ref[...] + sq_in[...])[:, :1] / features + 1e-06)
+    first.wait()
+    value = stream_ref[...].astype(jnp.float32) + (own_ref[...] + arrived[...]) * scale
+    rounded = value.astype(jnp.bfloat16)
+    resid[...] = rounded
+    value = rounded.astype(jnp.float32)
+    mine = jnp.broadcast_to(jnp.sum(value * value, axis=1, keepdims=True), sq_mine.shape)
+    sq_mine[...] = mine
+    third = remote(sq_mine, sq_two, pair_send.at[2], pair_recv.at[2], twin)
+    third.start()
+    third.wait()
+    inverse = lax.rsqrt((mine + sq_two[...])[:, :1] / width + 1e-06)
+    normed = (value * inverse * gain_ref[...]).astype(jnp.bfloat16)
+    rows = normed.shape[0] // 2
+    everything[head, frame, 0] = normed[:rows]
+    everything[head, frame, 1] = normed[rows:]
+    copies = []
+
+    def to_twin(source, half):
+        slot = everything.at[head, source, half]
+        copy = remote(slot, slot, twin_send.at[source, half], twin_recv.at[source, half], twin)
+        copy.start()
+        copies.append((copy, source, half))
+
+    ring_start = [0]
+    ring_gather(lambda source, half: everything.at[head, source, half], place, n,
+                ring_send, ring_recv, to_twin)
+    to_twin(frame, 0)
+    to_twin(frame, 1)
+    for copy, source, half in copies:
+        copy.wait_send()
+    for copy, source, half in copies:
+        slot = everything.at[1 - head, source, half]
+        remote(slot, slot, twin_send.at[source, half], twin_recv.at[source, half],
+               twin).wait_recv()
+
+
+def third_kernel(n, own_ref, other_ref, resid_ref, out_ref, twin_in, send_buf, recv_buf,
+                 twin_send, twin_recv, ring_send, ring_recv):
+    frame, head = lax.axis_index("frame"), lax.axis_index("head")
+    place = ring_place(frame, n)
+    twin = {"head": 1 - head}
+    ends = [ring_frame((place + 1) % n, n), ring_frame((place + n - 1) % n, n)]
+    far = n // 2
+    greet([twin, {"frame": ends[0]}, {"frame": ends[1]}])
+    schedule = [
+        (step, way, half)
+        for step in range(1, far + 1)
+        for half in range(2)
+        for way in range(2)
+        if step > 1 or way == half
+    ]
+
+    def target(step, way):
+        ahead = far + 1 - step
+        return ring_frame((place + (ahead if way == 0 else n - ahead)) % n, n)
+
+    twins = {}
+    order = [(far, half) for half in range(2)]
+    order = []
+    for step, way, half in schedule:
+        key = (1 if step == 1 else way, far + 1 - step, half)
+        if key not in order:
+            order.append(key)
+    order += [(0, 0, 0), (0, 0, 1)]
+
+    def frame_of(key):
+        way, ahead, half = key
+        return ring_frame((place + (ahead if way == 0 else n - ahead)) % n, n)
+
+    for at, key in enumerate(order):
+        q = frame_of(key)
+        copy = remote(other_ref.at[q, key[2]], twin_in.at[q, key[2]], twin_send.at[at],
+                      twin_recv.at[at], twin)
+        copy.start()
+        twins[key] = copy
+
+    def term(key):
+        twins[key].wait()
+        q = frame_of(key)
+        return own_ref[q, key[2]] + twin_in[q, key[2]].astype(jnp.float32)
+
+    def arrival(step, way, half):
+        slot = recv_buf.at[way, step - 1, half]
+        remote(slot, slot, ring_send.at[way, step, half], ring_recv.at[way, step, half],
+               {"frame": ends[way]}).wait_recv()
+        return recv_buf[way, step - 1, half].astype(jnp.float32)
+
+    started = []
+    for step, way, half in schedule:
+        key = (1 if step == 1 else way, far + 1 - step, half)
+        total = term(key)
+        if step > 2 or (step == 2 and way == half):
+            total = total + arrival(step - 1, way, half)
+        send_buf[way, step - 1, half] = total.astype(jnp.bfloat16)
+        copy = remote(send_buf.at[way, step - 1, half], recv_buf.at[way, step - 1, half],
+                      ring_send.at[way, step, half], ring_recv.at[way, step, half],
+                      {"frame": ends[way]})
+        copy.start()
+        started.append(copy)
+    rows = out_ref.shape[0] // 2
+    for half in range(2):
+        total = term((0, 0, half))
+        for way in range(2):
+            total = total + arrival(far, way, half)
+        block = resid_ref[half * rows:(half + 1) * rows].astype(jnp.float32)
+        out_ref[half * rows:(half + 1) * rows] = (block + total).astype(jnp.bfloat16)
+    for copy in started:
+        copy.wait_send()
+
+
+VMEM = pl.BlockSpec(memory_space=pltpu.VMEM)
+
+
+def call(kernel, ident, outs, scratch, *args):
+    return pl.pallas_call(
+        kernel,
+        out_shape=outs,
+        in_specs=[VMEM] * len(args),
+        out_specs=[VMEM] * len(outs) if isinstance(outs, (list, tuple)) else VMEM,
+        scratch_shapes=scratch,
+        compiler_params=pltpu.CompilerParams(
+            collective_id=ident, has_side_effects=True, vmem_limit_bytes=48 * 2**20
+        ),
+    )(*args)
+
+
+def token_body(
+    stream, queries, key_rows, value_rows, attn_gain, w_out, ffn_gain, w_up, conv_taps, w_down
+):
+    n = lax.axis_size("frame")
+    frame, head = lax.axis_index("frame"), lax.axis_index("head")
+    f32, bf16 = jnp.float32, jnp.bfloat16
+    tokens = queries.shape[0]
+    heads_here = queries.shape[1] // HEAD_DIM
+    dma = pltpu.SemaphoreType.DMA
+    far = n // 2
+    ring = [dma((2, far + 1, 2)), dma((2, far + 1, 2))]
+
+    def split(x):
+        return x.reshape(tokens, heads_here, HEAD_DIM)
+
+    pad = 128
+    qpos = split(jnp.maximum(queries, 0))
+    kpos = split(jnp.maximum(key_rows, 0))
+    ones = jnp.zeros((tokens, heads_here, pad - HEAD_DIM), bf16).at[:, :, 0].set(1)
+    values = jnp.concatenate([split(value_rows), ones], axis=2)
+    own_state = jnp.einsum("thb,thc->hbc", kpos, values, preferred_element_type=f32)
+    sent = own_state.astype(bf16).reshape(2, heads_here * HEAD_DIM // 2, pad)
+
+    up_rows, hidden = w_up.shape
+    part = hidden // n
+    out_cols = w_down.shape[1]
+    up_blocks = w_up.reshape(up_rows, n, part).transpose(1, 0, 2)
+    down_blocks = w_down.reshape(n, part, out_cols)
+    states, up_all, down_all = call(
+        functools.partial(first_kernel, n), 0,
+        [
+            jax.ShapeDtypeStruct((n,) + sent.shape, bf16),
+            jax.ShapeDtypeStruct((n, up_rows, part), bf16),
+            jax.ShapeDtypeStruct((n, part, out_cols), bf16),
+        ],
+        [dma((3,))] + ring + [dma((2, n)), dma((2, n))],
+        sent, up_blocks, down_blocks,
+    )
+    w_out_all = lax.all_gather(w_out, "frame", axis=1, tiled=True)
+    earlier = (jnp.arange(n) < frame).astype(f32)
+    state = own_state + jnp.sum(
+        states.astype(f32) * earlier[:, None, None, None], axis=0
+    ).reshape(own_state.shape)
+    both = jnp.einsum(
+        "thb,hbc->thc", qpos.astype(f32), state, precision=lax.Precision.HIGHEST
+    )
+    attended = both[:, :, :HEAD_DIM] / (both[:, :, HEAD_DIM:HEAD_DIM + 1] + 1e-06)
+    attended = attended.reshape(tokens, heads_here * HEAD_DIM)
+    squares = jnp.broadcast_to(
+        jnp.sum(attended * attended, axis=1, keepdims=True), (tokens, 128)
+    )
+    gained = (attended * attn_gain).astype(bf16)
+    width = stream.shape[1]
+    half_out = [
+        jnp.dot(gained, lax.dynamic_slice_in_dim(w_out_all, at * width, width, 1),
+                preferred_element_type=f32)
+        for at in (head, 1 - head)
+    ]
+    gain_here = lax.dynamic_slice_in_dim(ffn_gain, head * width, width, 0)[None]
+    everything, resid = call(
+        functools.partial(second_kernel, n, HEADS * HEAD_DIM, D), 1,
+        [
+            jax.ShapeDtypeStruct((2, n, 2, tokens // 2, width), bf16),
+            jax.ShapeDtypeStruct((tokens, width), bf16),
+        ],
+        [
+            pltpu.VMEM((tokens, width), f32),
+            pltpu.VMEM((tokens, 128), f32),
+            pltpu.VMEM((tokens, 128), f32),
+            pltpu.VMEM((tokens, 128), f32),
+            dma((3,)), dma((3,)),
+        ] + ring + [dma((n, 2)), dma((n, 2))],
+        half_out[0], half_out[1], squares, stream, gain_here,
+    )
+    ffn_in = everything.reshape(2, n * tokens, width)
+    up_full = up_all.reshape(2, width, part)
+    up_value = jnp.dot(ffn_in[0], up_full[0], preferred_element_type=f32) + jnp.dot(
+        ffn_in[1], up_full[1], preferred_element_type=f32
+    )
+    hidden_all = jax.nn.silu(up_value).astype(bf16).reshape(n * tokens // TPF, TPF, part)
+    padded = jnp.pad(hidden_all, ((1, 1), (0, 0), (0, 0))).astype(f32)
+    taps = lax.dynamic_slice_in_dim(conv_taps, frame * part, part, 1)
+    mixed = taps[0] * padded[:-2] + taps[1] * padded[1:-1] + taps[2] * padded[2:]
+    mixed = mixed.astype(bf16).reshape(n * tokens, part)
+
+    def down_half(at):
+        blocks = lax.dynamic_slice_in_dim(down_all, at * (n // 2), n // 2, 0)
+        return blocks.transpose(1, 0, 2).reshape(part, width)
+
+    own = jnp.dot(mixed, down_half(head), preferred_element_type=f32)
+    other = jnp.dot(mixed, down_half(1 - head), preferred_element_type=f32).astype(bf16)
+    shape = (n, 2, tokens // 2, width)
+    return call(
+        functools.partial(third_kernel, n), 2,
+        jax.ShapeDtypeStruct((tokens, width), bf16),
+        [
+            pltpu.VMEM(shape, bf16),
+            pltpu.VMEM((2, far, 2, tokens // 2, width), bf16),
+            pltpu.VMEM((2, far, 2, tokens // 2, width), bf16),
+            dma((2 * n,)), dma((2 * n,)),
+        ] + ring,
+        own.reshape(shape), other.reshape(shape), resid,
+    )
+
+
 def solution(mesh):
     in_specs = (
         P(("groups", "frame"), "head"),
@@ -128,4 +480,22 @@
         P("head", "frame"),
     )
     out_specs = P(("groups", "frame"), "head")
-    return jax.shard_map(body, mesh=mesh, in_specs=in_specs, out_specs=out_specs, check_vma=False)
+    frames, heads = mesh.shape["frame"], mesh.shape["head"]
+
+    def step(*args):
+        group_tokens = args[0].shape[0] // mesh.shape["groups"]
+        width, hidden = args[7].shape
+        tokens_move = (
+            group_tokens <= hidden
+            and heads == 2
+            and frames % 2 == 0
+            and frames >= 4
+            and hidden % (heads * frames) == 0
+            and width % (heads * frames) == 0
+        )
+        return jax.shard_map(
+            token_body if tokens_move else body,
+            mesh=mesh, in_specs=in_specs, out_specs=out_specs, check_vma=False,
+        )(*args)
+
+    return step

time: 409 us -> 229 us (0.56)
  waiting for transfers between devices: 317 us -> 0.71 us
  Pallas kernels: 0 us -> 172 us
  blocking collectives: 39.6 us -> 0 us
  local copies, waits for them, and re-layouts: 0.31 us -> 23.8 us
  other arithmetic: 14.3 us -> 4.6 us
  matrix products: 19.3 us -> 13.7 us
    all_gather x4 -> x1, waiting for transfers between devices: 279 us -> 0.01 us  [token_body(): w_out_all = lax.all_gather(w_out, 'frame', axis=1, tiled=True)]
    pallas_call x0 -> x3, Pallas kernels: none -> 172 us  [call(): pl.pallas_call(kernel, out_shape=outs, in_specs=[VMEM] * len(args), out_s...]
    all_gather x2 -> x0, blocking collectives: 34.7 us -> none  [the longest x1 32.4 us: prefix(): everything = jax.tree.map(lambda part: lax.all_gather(part, axis), x)]
    ppermute x2 -> x0, waiting for transfers between devices: 23.9 us -> none  [the longest x1 23.9 us: padded_2(): lax.ppermute(lax.slice_in_dim(block, block.shape[dim] - width, None, axis...]
    reduce_scatter x2 -> x0, waiting for transfers between devices: 12.8 us -> none  [the longest x1 6.82 us: body(): lax.psum_scatter(ffn_terms, 'head', scatter_dimension=1, tiled=True)]
    reshape x0 -> x6, local copies, waits for them, and re-layouts: none -> 9.3 us  [the longest x2 4.87 us: token_body(): down_blocks = w_down.reshape(n, part, out_cols)]
    select_n x16 -> x0, other arithmetic: 8.52 us -> none  [hop(): return jax.tree.map(lambda a, b: jnp.where(reached, a, b), new, before)]
    dot_general x6 -> x8, matrix products: 19.3 us -> 13.7 us  [the longest x1 4.07 us: token_body(): own = jnp.dot(mixed, down_half(head), preferred_element_type=f32)]
  transfers between devices with their start and end apart: 8 -> 1, of which waited for: 7 -> 0; matrix products, arithmetic and copies ran while one was open for 5% -> 8% of each run, Pallas kernels for 0% -> 46%
where the time goes in v1:
time: 229 us
  Pallas kernels  172 us (75%)
  local copies, waits for them, and re-layouts  23.8 us (10%)
  matrix products  13.7 us (6%)
  between operations  13.7 us (6%)
  other arithmetic  4.6 us (2%)
    pallas_call x3, Pallas kernels, call(): pl.pallas_call(kernel, out_shape=outs, in_specs=[VMEM] * len(args), out_s...  172 us
    reshape x2, local copies, waits for them, and re-layouts, token_body(): down_blocks = w_down.reshape(n, part, out_cols)  4.87 us
  transfers between devices with their start and end apart: 1, of which 0 were waited for; matrix products, arithmetic and copies ran while one was open for 8% of the time, Pallas kernels for 46%

profile of v1, /device:TPU:0, one launch (start us, length us, event | category | flops | bytes accessed | tf_op | source)
XLA Modules:
  0.0 228.8 jit_solution(16713556490548180918)
XLA Ops:
  6.5 0.0 all-gather.2.cloned.1.call-start
  6.5 0.7 all-gather.2.cloned.1.call-update
  7.3 0.8 dynamic_slice.21
  8.1 1.1 copy.18
  9.1 1.2 copy.23.stream_ref
  10.3 3.1 %reshape.93 = bf16[280,8,210]{2,1,0:T(8,128)(2,1)S(1)} reshape(bf16[280,1680]{1,0:T(8,128)(2,1)} %param.19) | data formatting | bytes 1881600 | tf_op jit(solution)/shard_map/reshape | solution.py:390
  13.4 0.2 copy.39
  13.6 0.0 copy-start.5
  13.7 0.0 copy-start.4
  13.7 3.1 %reshape.94 = bf16[8,210,280]{1,0,2:T(8,128)(2,1)S(1)} reshape(bf16[1680,280]{0,1:T(8,128)(2,1)} %param.21) | data formatting | bytes 1881600 | tf_op jit(solution)/shard_map/reshape | solution.py:391
  16.8 1.7 copy.20.down_ref
  18.5 0.0 copy-done.5
  18.6 0.0 copy-done.4
  18.6 0.0 copy-start.6
  18.6 0.3 fusion.18
  18.9 105.8 %shard_map.100 = (bf16[8,2,280,128]{3,2,1,0:T(8,128)(2,1)S(1)}, bf16[8,280,210]{2,1,0:T(8,128)(2,1)S(1)}, bf16[8,210,280]{2,1,0:T(8,128)(2,1)S(1)}) custom-call(bf16[2,280,128]{2,1,0:T(8,128)(2,1)S(1)} %bitcast.62, bf16[8,280,210]{2,1,0:T(8,128)(2,1)S(1)} %bitcast.61, bf16[8,210,280]{2,1,0:T(8,128)(2,1)} %copy.20.down_ref), custom_call_target="tpu_custom_call" | custom-call | tf_op jit(solution)/shard_map/pallas_call | solution.py:352
  124.7 0.0 copy-start
  124.7 1.0 copy-done
  125.7 0.3 multiply_reduce_fusion
  126.0 1.2 convolution_bitcast_fusion
  127.2 0.7 slice_add_fusion
  128.0 0.1 dynamic-slice_bitcast_fusion
  128.1 0.3 copy.27
  128.4 1.1 copy.25
  129.5 0.9 constant_dynamic-slice_fusion
  130.4 1.1 multiply_reduce_fusion.1
  131.5 0.1 fusion.7
  131.6 0.0 copy-done.1
  131.6 0.9 fusion.17
  132.5 2.0 fusion.2.own_ref
  134.5 2.0 fusion.other_ref
  136.5 0.1 broadcast_in_dim.4.sq_ref
  136.6 35.2 %shard_map.101 = (bf16[2,8,2,64,1120]{4,3,2,1,0:T(8,128)(2,1)}, bf16[128,1120]{1,0:T(8,128)(2,1)S(1)}) custom-call(f32[128,1120]{1,0:T(8,128)S(1)} %fusion.2.own_ref, f32[128,1120]{1,0:T(8,128)S(1)} %fusion.other_ref, f32[128,128]{1,0:T(8,128)S(1)} %broadcast_in_dim.4.sq_ref, bf16[128,1120]{1,0:T(8,128)(2,1)S(1)} %copy.23.stream_ref, ...), custom_call_target="tpu_custom_call" | custom-call | tf_op jit(solution)/shard_map/pallas_call | solution.py:352
  171.8 2.7 %fusion.16 = (bf16[1,8,2,64,1120]{4,3,2,1,0:T(8,128)(2,1)S(1)}, bf16[1,8,2,64,1120]{4,3,2,1,0:T(8,128)(2,1)S(1)}) fusion(bf16[2,8,2,64,1120]{4,3,2,1,0:T(8,128)(2,1)} %get-tuple-element.23), kind=kLoop, calls=%fused_computation.38 | loop fusion | bytes 9175040 | tf_op jit(solution)/shard_map/slice | solution.py:441
  174.5 0.9 fusion.19
  175.5 0.1 copy-done.3
  175.6 1.1 multiply_convert_fusion
  176.7 0.1 copy.35
  176.8 0.2 pad_convert_fusion
  177.0 1.0 fusion.33
  178.0 1.2 fusion.5
  179.2 0.1 copy.36
  179.3 1.1 copy.24
  180.4 2.1 convolution_convert_fusion
  182.6 3.0 %copy.28 = bf16[1024,1120]{1,0:T(8,128)(2,1)S(1)} copy(bf16[1024,1120]{0,1:T(8,128)(2,1)} %convolution_convert_fusion) | data formatting | bytes 4587520 | tf_op jit(solution)/shard_map/convert_element_type | solution.py:454
  185.6 4.1 %fusion.20.own_ref = f32[8,2,64,1120]{3,2,1,0:T(8,128)} fusion(bf16[8,2,64,210]{3,2,1,0:T(8,128)(2,1)} %bitcast.69, bf16[210,1120,1,1]{0,1,3,2:T(8,128)(2,1)S(1)} %bitcast.67), kind=kOutput, calls=%fused_computation.42 | convolution fusion | flops 481689600 | bytes 5488000 | tf_op jit(solution)/shard_map/dot_general | solution.py:453
  189.7 31.3 %shard_map.102 = bf16[128,1120]{1,0:T(8,128)(2,1)S(1)} custom-call(f32[8,2,64,1120]{3,2,1,0:T(8,128)} %fusion.20.own_ref, bf16[8,2,64,1120]{3,2,1,0:T(8,128)(2,1)S(1)} %bitcast.60, bf16[128,1120]{1,0:T(8,128)(2,1)S(1)} %get-tuple-element.26.resid_ref), custom_call_target="tpu_custom_call" | custom-call | tf_op jit(solution)/shard_map/pallas_call | solution.py:352
  221.1 0.9 copy.29
  (15 shorter events, 0.1 us)
Async XLA Ops:
  6.5 126.0 %all-gather.2.cloned.1.call-start = ((), (), s32[]{:S(2)}) async-start(), calls=%async_computation | async-start | bytes 3225600 | tf_op jit(solution)/shard_map/all_gather | solution.py:402
  13.6 4.9 %copy-start.5 = (bf16[128,560]{0,1:T(8,128)(2,1)S(1)}, bf16[128,560]{0,1:T(8,128)(2,1)}, u32[]{:S(2)}) copy-start(bf16[128,560]{0,1:T(8,128)(2,1)} %param.14) | copy-start | bytes 430084
  13.7 4.9 %copy-start.4 = (bf16[128,5,16]{2,0,1:T(8,128)(2,1)S(1)}, bf16[128,5,16]{2,0,1:T(8,128)(2,1)}, u32[]{:S(2)}) copy-start(bf16[128,5,16]{2,0,1:T(8,128)(2,1)} %constant.55.clone.1) | copy-start | bytes 61444
  18.6 107.4 %copy-start.6 = (bf16[128,560]{0,1:T(8,128)(2,1)S(1)}, bf16[128,560]{0,1:T(8,128)(2,1)}, u32[]{:S(2)}) copy-start(bf16[128,560]{0,1:T(8,128)(2,1)} %param.13) | copy-start | bytes 430084
  124.7 1.0 copy-start
  128.0 3.5 %copy-start.7 = (f32[560]{0:T(1024)S(1)}, f32[560]{0:T(1024)}, u32[]{:S(2)}) copy-start(f32[560]{0:T(1024)} %param.16) | copy-start | bytes 6724
  128.1 3.5 %copy-start.1 = (bf16[8,280,210]{2,1,0:T(8,128)(2,1)S(1)}, bf16[8,280,210]{2,1,0:T(8,128)(2,1)}, u32[]{:S(2)}) copy-start(bf16[8,280,210]{2,1,0:T(8,128)(2,1)} %copy-done) | copy-start | bytes 2822404
  174.5 1.1 copy-start.3
  182.6 3.1 %copy-start.2 = (bf16[210,4,280]{0,2,1:T(8,128)(2,1)S(1)}, bf16[210,4,280]{0,2,1:T(8,128)(2,1)}, u32[]{:S(2)}) copy-start(bf16[210,4,280]{0,2,1:T(8,128)(2,1)} %copy.25) | copy-start | bytes 1411204
Sparse Core Ops, SparseCore 0:
  9.5 93.8 all-gather.1

commit v2 on v1

--- a/solution.py
+++ b/solution.py
@@ -187,38 +187,109 @@
         copy.wait_send()
 
 
-def first_kernel(n, state_ref, up_ref, down_ref, states, up_out, down_out, here,
-                 ring_send, ring_recv, all_send, all_recv):
-    frame = lax.axis_index("frame")
+def first_kernel(n, state_ref, up_ref, down_ref, proj_ref, states, weights, proj, blocks, here,
+                 state_send, state_recv, proj_send, proj_recv, all_send, all_recv,
+                 over_send, over_recv):
+    frame, group = lax.axis_index("frame"), lax.axis_index("groups")
     place = ring_place(frame, n)
+    over = {"groups": 1 - group}
+    ends = [ring_frame((place + 1) % n, n), ring_frame((place + n - 1) % n, n)]
+    far = n // 2
+    part = weights.shape[3]
     local = [
         pltpu.make_async_copy(state_ref, states.at[frame], here.at[0]),
-        pltpu.make_async_copy(up_ref.at[frame], up_out.at[frame], here.at[1]),
-        pltpu.make_async_copy(down_ref.at[frame], down_out.at[frame], here.at[2]),
+        pltpu.make_async_copy(proj_ref, proj.at[frame], here.at[1]),
     ]
     for copy in local:
         copy.start()
-    greet([{"frame": (frame + k) % n} for k in range(1, n)])
+    for at, ref in enumerate((up_ref, down_ref)):
+        for j in range(n):
+            blocks[at, j] = ref[:, j * part:(j + 1) * part]
+    for at in range(2):
+        local.append(
+            pltpu.make_async_copy(blocks.at[at, frame], weights.at[at, frame], here.at[2 + at])
+        )
+        local[-1].start()
+    greet([{"frame": (frame + k) % n} for k in range(1, n)] + [over])
     local[0].wait()
-    pushes = []
-    for at, (src, dst) in enumerate(((up_ref, up_out), (down_ref, down_out))):
-        for k in range(1, n):
+    local[1].wait()
+
+    def origin(step, way):
+        back = step if way == 0 else n - step
+        return ring_frame((place + n - back) % n, n)
+
+    ring, pushed, swapped = [], [], []
+
+    def state_copy(step, way, half, source):
+        slot = states.at[source, half]
+        return remote(slot, slot, state_send.at[way, step, half], state_recv.at[way, step, half],
+                      {"frame": ends[way]})
+
+    def proj_copy(step, way, source):
+        slot = proj.at[source, group]
+        return remote(slot, slot, proj_send.at[way, step], proj_recv.at[way, step],
+                      {"frame": ends[way]})
+
+    def swap(slot, at):
+        copy = remote(slot, slot, over_send.at[at], over_recv.at[at], over)
+        copy.start()
+        swapped.append(copy)
+
+    ways = list(range(1, n))
+    ways.sort(key=lambda k: -min(k, n - k))
+    for step in range(1, far + 1):
+        for half in range(2):
+            for way in range(2):
+                if step == far and way != half:
+                    continue
+                if step > 1:
+                    state_copy(step - 1, way, half, origin(step - 1, way)).wait_recv()
+                copy = state_copy(step, way, half, origin(step - 1, way))
+                copy.start()
+                ring.append(copy)
+        for way in range(2):
+            if step > 1:
+                source = origin(step - 1, way)
+                proj_copy(step - 1, way, source).wait_recv()
+            if step < far or way == 0:
+                copy = proj_copy(step, way, origin(step - 1, way))
+                copy.start()
+                ring.append(copy)
+            if step > 1:
+                swap(proj.at[source, group], 2 * (step - 1) + way)
+        for k in ways[2 * (step - 1):2 * step]:
             target = (frame + k) % n
-            copy = remote(src.at[target], dst.at[frame], all_send.at[at, k],
-                          all_recv.at[at, k], {"frame": target})
-            pushes.append((copy, at, k))
-    for copy, at, k in pushes:
-        copy.start()
-    ring_gather(lambda source, half: states.at[source, half], place, n,
-                ring_send, ring_recv, lambda source, half: None)
-    for copy, at, k in pushes:
+            copy = remote(blocks.at[group, target], weights.at[group, frame], all_send.at[k],
+                          all_recv.at[k], {"frame": target})
+            copy.start()
+            pushed.append(copy)
+    for k in ways:
+        source = (frame + n - k) % n
+        slot = weights.at[group, source]
+        remote(slot, slot, all_send.at[k], all_recv.at[k], {"frame": source}).wait_recv()
+        swap(slot, 2 * far + k)
+    proj_copy(far, 0, origin(far, 0)).wait_recv()
+    swap(proj.at[origin(far, 0), group], 2 * far)
+    for half in range(2):
+        for way in range(2):
+            last = far if way == half else far - 1
+            state_copy(last, way, half, origin(last, way)).wait_recv()
+    for copy in ring + pushed:
         copy.wait_send()
-        source = (frame + n - k) % n
-        dst = (up_out, down_out)[at]
-        remote(dst.at[source], dst.at[source], all_send.at[at, k], all_recv.at[at, k],
-               {"frame": source}).wait_recv()
-    local[1].wait()
+
+    def swapped_in(slot, at):
+        remote(slot, slot, over_send.at[at], over_recv.at[at], over).wait_recv()
+
+    for step in range(1, far):
+        for way in range(2):
+            swapped_in(proj.at[origin(step, way), 1 - group], 2 * step + way)
+    swapped_in(proj.at[origin(far, 0), 1 - group], 2 * far)
+    for k in ways:
+        swapped_in(weights.at[1 - group, (frame + n - k) % n], 2 * far + k)
+    for copy in swapped:
+        copy.wait_send()
     local[2].wait()
+    local[3].wait()
 
 
 def second_kernel(n, features, width, own_ref, other_ref, sq_ref, stream_ref, gain_ref,
@@ -387,19 +458,19 @@
     up_rows, hidden = w_up.shape
     part = hidden // n
     out_cols = w_down.shape[1]
-    up_blocks = w_up.reshape(up_rows, n, part).transpose(1, 0, 2)
-    down_blocks = w_down.reshape(n, part, out_cols)
-    states, up_all, down_all = call(
+    states, weights, proj = call(
         functools.partial(first_kernel, n), 0,
         [
             jax.ShapeDtypeStruct((n,) + sent.shape, bf16),
-            jax.ShapeDtypeStruct((n, up_rows, part), bf16),
-            jax.ShapeDtypeStruct((n, part, out_cols), bf16),
+            jax.ShapeDtypeStruct((2, n, up_rows, part), bf16),
+            jax.ShapeDtypeStruct((n, 2, out_cols // 2, w_out.shape[0]), bf16),
         ],
-        [dma((3,))] + ring + [dma((2, n)), dma((2, n))],
-        sent, up_blocks, down_blocks,
-    )
-    w_out_all = lax.all_gather(w_out, "frame", axis=1, tiled=True)
+        [pltpu.VMEM((2, n, up_rows, part), bf16), dma((4,))] + ring
+        + [dma((2, far + 1)), dma((2, far + 1)), dma((n,)), dma((n,)), dma((2 * n,)), dma((2 * n,))],
+        sent, w_up, w_down.T, w_out.T.reshape(2, out_cols // 2, w_out.shape[0]),
+    )
+    up_all, down_all = weights[0], weights[1]
+    proj_t = proj.reshape(n * out_cols, w_out.shape[0])
     earlier = (jnp.arange(n) < frame).astype(f32)
     state = own_state + jnp.sum(
         states.astype(f32) * earlier[:, None, None, None], axis=0
@@ -414,9 +485,11 @@
     )
     gained = (attended * attn_gain).astype(bf16)
     width = stream.shape[1]
+    def against(x, y):
+        return lax.dot_general(x, y, (((1,), (1,)), ((), ())), preferred_element_type=f32)
+
     half_out = [
-        jnp.dot(gained, lax.dynamic_slice_in_dim(w_out_all, at * width, width, 1),
-                preferred_element_type=f32)
+        against(gained, lax.dynamic_slice_in_dim(proj_t, at * width, width, 0))
         for at in (head, 1 - head)
     ]
     gain_here = lax.dynamic_slice_in_dim(ffn_gain, head * width, width, 0)[None]
@@ -447,11 +520,12 @@
     mixed = mixed.astype(bf16).reshape(n * tokens, part)
 
     def down_half(at):
-        blocks = lax.dynamic_slice_in_dim(down_all, at * (n // 2), n // 2, 0)
-        return blocks.transpose(1, 0, 2).reshape(part, width)
-
-    own = jnp.dot(mixed, down_half(head), preferred_element_type=f32)
-    other = jnp.dot(mixed, down_half(1 - head), preferred_element_type=f32).astype(bf16)
+        return against(
+            mixed, lax.dynamic_slice_in_dim(down_all, at * (n // 2), n // 2, 0).reshape(width, part)
+        )
+
+    own = down_half(head)
+    other = down_half(1 - head).astype(bf16)
     shape = (n, 2, tokens // 2, width)
     return call(
         functools.partial(third_kernel, n), 2,
@@ -488,10 +562,12 @@
         tokens_move = (
             group_tokens <= hidden
             and heads == 2
+            and mesh.shape["groups"] == 2
             and frames % 2 == 0
             and frames >= 4
             and hidden % (heads * frames) == 0
             and width % (heads * frames) == 0
+            and args[5].shape[1] % (2 * frames) == 0
         )
         return jax.shard_map(
             token_body if tokens_move else body,

time: 229 us -> 203 us (0.89)
  Pallas kernels: 172 us -> 154 us
  between operations: 13.7 us -> 0.26 us
  other arithmetic: 4.6 us -> 12.1 us
    pallas_call x3, Pallas kernels: 172 us -> 154 us  [call(): pl.pallas_call(kernel, out_shape=outs, in_specs=[VMEM] * len(args), out_s...]
    unnamed x21 -> x23, local copies, waits for them, and re-layouts: 2.48 us -> 6.41 us
    convert_element_type x1, other arithmetic: 1.18 us -> 3.84 us  [token_body(): mixed = mixed.astype(bf16).reshape(n * tokens, part)]
    reshape x4 -> x2, local copies, waits for them, and re-layouts: 8.2 us -> 5.71 us  [the longest x1 4.66 us: token_body(): proj_t = proj.reshape(n * out_cols, w_out.shape[0])]
  transfers between devices with their start and end apart: 1 -> 0, of which waited for: 0 -> 0; matrix products, arithmetic and copies ran while one was open for 8% -> 0% of each run, Pallas kernels for 46% -> 0%
where the time goes in v2:
time: 203 us; the launch traced here: 202 us
  Pallas kernels  154 us (76%)
  local copies, waits for them, and re-layouts  22.7 us (11%)
  matrix products  12.9 us (6%)
  other arithmetic  12.1 us (6%)
    pallas_call x3, Pallas kernels, call(): pl.pallas_call(kernel, out_shape=outs, in_specs=[VMEM] * len(args), out_s...  154 us
    dot_general x4, matrix products, against(): lax.dot_general(x, y, (((1,), (1,)), ((), ())), preferred_element_type=f32)  9.2 us
    unnamed x23, local copies, waits for them, and re-layouts  6.41 us
    reshape x1, local copies, waits for them, and re-layouts, token_body(): proj_t = proj.reshape(n * out_cols, w_out.shape[0])  4.66 us

profile of v2, /device:TPU:0, one launch (start us, length us, event | category | flops | bytes accessed | tf_op | source)
XLA Modules:
  0.0 201.8 jit_solution(16720649041094447990)
XLA Ops:
  0.0 1.1 copy.17
  1.1 0.9 broadcast_maximum_fusion.1
  2.0 1.2 fusion.18
  3.2 1.1 reshape.96.proj_ref
  4.3 0.0 copy-start.2
  4.3 1.2 copy-done.2
  5.5 1.2 copy-done.3
  6.7 78.2 %shard_map.100 = (bf16[8,2,280,128]{3,2,1,0:T(8,128)(2,1)S(1)}, bf16[2,8,280,210]{3,2,1,0:T(8,128)(2,1)S(1)}, bf16[8,2,140,560]{3,2,1,0:T(8,128)(2,1)}) custom-call(bf16[2,280,128]{2,1,0:T(8,128)(2,1)S(1)} %bitcast.55, bf16[280,1680]{1,0:T(8,128)(2,1)S(1)} %copy-done.2, bf16[280,1680]{1,0:T(8,128)(2,1)S(1)} %bitcast.54, ...), custom_call_target="tpu_custom_call" | custom-call | tf_op jit(solution)/shard_map/pallas_call | solution.py:423
  84.9 0.0 copy-start.1
  84.9 1.0 copy-done.1
  85.9 1.6 multiply_reduce_fusion
  87.5 0.9 broadcast_maximum_fusion
  88.4 0.5 convolution_bitcast_fusion
  88.9 0.1 multiply_reduce_fusion.1
  89.0 0.0 copy-done.8
  89.0 0.1 fusion.7
  89.2 0.0 copy-start.6
  89.2 4.7 %reshape.100 = bf16[2240,560]{1,0:T(8,128)(2,1)} reshape(bf16[8,2,140,560]{3,2,1,0:T(8,128)(2,1)} %get-tuple-element.23) | data formatting | bytes 5017600 | tf_op jit(solution)/shard_map/reshape | solution.py:473
  93.9 0.0 copy-done.6
  93.9 2.0 fusion.other_ref
  95.8 2.1 %fusion.2.own_ref = f32[128,1120]{1,0:T(8,128)S(1)} fusion(bf16[128,560]{0,1:T(8,128)(2,1)} %copy-done.6, bf16[2240,560]{1,0:T(8,128)(2,1)} %reshape.100, s32[]{:T(128)S(6)} %select_n.17), kind=kOutput, calls=%fused_computation.4 | convolution fusion | flops 160563200 | bytes 2150404 | tf_op jit(solution)/shard_map/dot_general | solution.py:489
  97.9 0.0 copy-done.7
  97.9 0.1 dynamic_slice.21
  98.0 0.1 broadcast_in_dim.4.sq_ref
  98.1 1.8 copy.20.stream_ref
  99.9 1.0 copy-done
  100.9 43.8 %shard_map.101 = (bf16[2,8,2,64,1120]{4,3,2,1,0:T(8,128)(2,1)}, bf16[128,1120]{1,0:T(8,128)(2,1)S(1)}) custom-call(f32[128,1120]{1,0:T(8,128)S(1)} %fusion.2.own_ref, f32[128,1120]{1,0:T(8,128)S(1)} %fusion.other_ref, f32[128,128]{1,0:T(8,128)S(1)} %broadcast_in_dim.4.sq_ref, bf16[128,1120]{1,0:T(8,128)(2,1)S(1)} %copy-done, ...), custom_call_target="tpu_custom_call" | custom-call | tf_op jit(solution)/shard_map/pallas_call | solution.py:423
  144.7 0.0 copy-start.4
  144.7 3.0 %fusion.16 = (bf16[1,8,2,64,1120]{4,3,2,1,0:T(8,128)(2,1)S(1)}, bf16[1,8,2,64,1120]{4,3,2,1,0:T(8,128)(2,1)S(1)}) fusion(bf16[2,8,2,64,1120]{4,3,2,1,0:T(8,128)(2,1)} %get-tuple-element.24), kind=kLoop, calls=%fused_computation.37 | loop fusion | bytes 9175040 | tf_op jit(solution)/shard_map/slice | solution.py:514
  147.7 0.0 copy-done.4
  147.7 0.1 fusion.17
  147.8 0.9 fusion.19
  148.8 1.1 multiply_convert_fusion
  149.8 0.1 copy.30
  150.0 1.4 pad_convert_fusion
  151.3 0.9 constant_dynamic-slice_fusion
  152.2 3.2 %fusion.33 = bf16[210,8,128]{2,1,0:T(8,128)(2,1)S(1)} fusion(f32[10,128,210]{1,0,2:T(8,128)} %pad_convert_fusion, f32[210]{0:T(256)S(1)} %bitcast.77, f32[210]{0:T(256)S(1)} %bitcast.75, f32[210]{0:T(256)S(1)} %bitcast.73), kind=kLoop, calls=%fused_computation.42 | loop fusion | flops 1290240 | bytes 3013080
  155.4 0.1 copy.31
  155.5 0.1 slice.77
  155.6 0.1 constant_dynamic-slice_fusion.1
  155.7 2.1 %convolution_convert_fusion = bf16[1024,1120]{0,1:T(8,128)(2,1)} fusion(bf16[1024,210]{0,1:T(8,128)(2,1)S(1)} %bitcast.57, bf16[1120,210]{1,0:T(8,128)(2,1)S(1)} %bitcast.59), kind=kOutput, calls=%fused_computation | convolution fusion | flops 482836480 | bytes 3194240 | tf_op jit(solution)/shard_map/dot_general | solution.py:489
  157.8 3.0 %copy.23 = bf16[1024,1120]{1,0:T(8,128)(2,1)S(1)} copy(bf16[1024,1120]{0,1:T(8,128)(2,1)} %convolution_convert_fusion) | data formatting | bytes 4587520 | tf_op jit(solution)/shard_map/convert_element_type | solution.py:528
  160.8 3.8 %fusion.5 = bf16[8,128,210]{1,0,2:T(8,128)(2,1)} fusion(f32[10,128,210]{1,0,2:T(8,128)} %pad_convert_fusion, f32[210]{0:T(256)S(1)} %bitcast.78, f32[210]{0:T(256)S(1)} %bitcast.76, f32[210]{0:T(256)S(1)} %bitcast.74), kind=kLoop, calls=%fused_computation.11 | loop fusion | flops 1290240 | bytes 3013080 | tf_op jit(solution)/shard_map/convert_element_type | solution.py:520
  164.6 1.3 copy.21
  165.9 0.0 copy-start.5
  165.9 3.0 %fusion.20.own_ref = f32[8,2,64,1120]{3,2,1,0:T(8,128)} fusion(bf16[8,2,64,210]{3,2,1,0:T(8,128)(2,1)S(1)} %bitcast.62, bf16[1120,210,1,1]{1,0,3,2:T(8,128)(2,1)S(1)} %bitcast.61), kind=kOutput, calls=%fused_computation.41 | convolution fusion | flops 481689600 | bytes 5488000 | tf_op jit(solution)/shard_map/dot_general | solution.py:489
  169.0 31.9 %shard_map.102 = bf16[128,1120]{1,0:T(8,128)(2,1)S(1)} custom-call(f32[8,2,64,1120]{3,2,1,0:T(8,128)} %fusion.20.own_ref, bf16[8,2,64,1120]{3,2,1,0:T(8,128)(2,1)S(1)} %bitcast.53, bf16[128,1120]{1,0:T(8,128)(2,1)S(1)} %copy-done.5), custom_call_target="tpu_custom_call" | custom-call | tf_op jit(solution)/shard_map/pallas_call | solution.py:423
  200.9 0.9 copy.24
  (11 shorter events, 0.1 us)
Async XLA Ops:
  4.3 1.2 copy-start.2
  5.5 1.2 copy-start.3
  6.7 82.3 %copy-start.8 = (f32[560]{0:T(1024)S(1)}, f32[560]{0:T(1024)}, u32[]{:S(2)}) copy-start(f32[560]{0:T(1024)} %param.16) | copy-start | bytes 6724
  84.9 1.0 copy-start.1
  89.2 4.7 %copy-start.6 = (bf16[128,560]{0,1:T(8,128)(2,1)}, bf16[128,560]{0,1:T(8,128)(2,1)S(1)}, u32[]{:S(2)}) copy-start(bf16[128,560]{0,1:T(8,128)(2,1)S(1)} %fusion.7) | copy-start | bytes 430084
  93.9 4.0 %copy-start.7 = (f32[2240]{0:T(1024)S(1)}, f32[2240]{0:T(1024)}, u32[]{:S(2)}) copy-start(f32[2240]{0:T(1024)} %param.18) | copy-start | bytes 26884
  99.9 1.0 copy-start
  144.7 3.0 %copy-start.4 = (bf16[128,1120]{1,0:T(8,128)(2,1)}, bf16[128,1120]{1,0:T(8,128)(2,1)S(1)}, u32[]{:S(2)}) copy-start(bf16[128,1120]{1,0:T(8,128)(2,1)S(1)} %get-tuple-element.26.resid_ref) | copy-start | bytes 860164
  165.9 3.0 %copy-start.5 = (bf16[128,1120]{1,0:T(8,128)(2,1)S(1)}, bf16[128,1120]{1,0:T(8,128)(2,1)}, u32[]{:S(2)}) copy-start(bf16[128,1120]{1,0:T(8,128)(2,1)} %copy-done.4) | copy-start | bytes 860164

commit v3 on v2

--- a/solution.py
+++ b/solution.py
@@ -156,7 +156,7 @@
     ]
 
 
-def ring_gather(buffer, place, n, send, recv, on_arrival):
+def ring_gather(buffer, place, n, send, recv, on_arrival, after_step):
     ends = [ring_frame((place + 1) % n, n), ring_frame((place + n - 1) % n, n)]
     started = []
 
@@ -179,15 +179,20 @@
                       {"frame": ends[way]})
         copy.start()
         started.append(copy)
-    for step, way, half in ring_steps(n):
-        last = n // 2 if way == half else n // 2 - 1
-        if step == last:
-            arrive(step, way, half)
-    for copy in started:
-        copy.wait_send()
-
-
-def first_kernel(n, state_ref, up_ref, down_ref, proj_ref, states, weights, proj, blocks, here,
+        if way == 1 and half == 1:
+            if step == n // 2:
+                arrive(step - 1, 0, 1)
+                arrive(step - 1, 1, 0)
+            after_step([ring_frame(place, n)] if step == 1 else
+                       [origin(step - 1, 0), origin(step - 1, 1)])
+    for way in range(2):
+        arrive(n // 2, way, way)
+    after_step([origin(n // 2, 0)])
+    return started
+
+
+def first_kernel(n, state_ref, up_ref, down_ref, proj_ref, states, weights, merged, proj,
+                 blocks, here,
                  state_send, state_recv, proj_send, proj_recv, all_send, all_recv,
                  over_send, over_recv):
     frame, group = lax.axis_index("frame"), lax.axis_index("groups")
@@ -284,6 +289,11 @@
         for way in range(2):
             swapped_in(proj.at[origin(step, way), 1 - group], 2 * step + way)
     swapped_in(proj.at[origin(far, 0), 1 - group], 2 * far)
+    count = proj.shape[2]
+    for at in range(n):
+        for half in range(2):
+            first_row = (2 * at + half) * count
+            merged[first_row:first_row + count] = proj[at, half]
     for k in ways:
         swapped_in(weights.at[1 - group, (frame + n - k) % n], 2 * far + k)
     for copy in swapped:
@@ -293,13 +303,20 @@
 
 
 def second_kernel(n, features, width, own_ref, other_ref, sq_ref, stream_ref, gain_ref,
-                  everything, resid, arrived, sq_in, sq_mine, sq_two,
-                  pair_send, pair_recv, ring_send, ring_recv, twin_send, twin_recv):
+                  up_ref, down_ref, taps_ref, out_ref,
+                  everything, resid, arrived, sq_in, sq_mine, sq_two, hidden, mixed, theirs,
+                  twin_in, send_buf, recv_buf,
+                  pair_send, pair_recv, ring_send, ring_recv, twin_send, twin_recv,
+                  sum_twin_send, sum_twin_recv, sum_send, sum_recv):
     frame, head = lax.axis_index("frame"), lax.axis_index("head")
     place = ring_place(frame, n)
     twin = {"head": 1 - head}
-    greet([twin, {"frame": ring_frame((place + 1) % n, n)},
-           {"frame": ring_frame((place + n - 1) % n, n)}])
+    ends = [ring_frame((place + 1) % n, n), ring_frame((place + n - 1) % n, n)]
+    far = n // 2
+    rows = stream_ref.shape[0] // 2
+    hidden[0] = jnp.zeros_like(hidden[0])
+    hidden[n + 1] = jnp.zeros_like(hidden[0])
+    greet([twin, {"frame": ends[0]}, {"frame": ends[1]}])
     first = remote(other_ref, arrived, pair_send.at[0], pair_recv.at[0], twin)
     second = remote(sq_ref, sq_in, pair_send.at[1], pair_recv.at[1], twin)
     second.start()
@@ -318,7 +335,6 @@
     third.wait()
     inverse = lax.rsqrt((mine + sq_two[...])[:, :1] / width + 1e-06)
     normed = (value * inverse * gain_ref[...]).astype(jnp.bfloat16)
-    rows = normed.shape[0] // 2
     everything[head, frame, 0] = normed[:rows]
     everything[head, frame, 1] = normed[rows:]
     copies = []
@@ -327,93 +343,112 @@
         slot = everything.at[head, source, half]
         copy = remote(slot, slot, twin_send.at[source, half], twin_recv.at[source, half], twin)
         copy.start()
-        copies.append((copy, source, half))
-
-    ring_start = [0]
-    ring_gather(lambda source, half: everything.at[head, source, half], place, n,
-                ring_send, ring_recv, to_twin)
+        copies.append(copy)
+
+    def up_blocks(sources):
+        for source in sources:
+            for half in range(2):
+                slot = everything.at[1 - head, source, half]
+                remote(slot, slot, twin_send.at[source, half], twin_recv.at[source, half],
+                       twin).wait_recv()
+            total = None
+            for at in range(2):
+                block = jnp.concatenate(
+                    [everything[at, source, 0], everything[at, source, 1]], axis=0
+                )
+                term = jnp.dot(block, up_ref[at], preferred_element_type=jnp.float32)
+                total = term if total is None else total + term
+            act = total / (1.0 + jnp.exp(-total))
+            hidden[source + 1] = act.astype(jnp.bfloat16).astype(jnp.float32)
+
     to_twin(frame, 0)
     to_twin(frame, 1)
-    for copy, source, half in copies:
-        copy.wait_send()
-    for copy, source, half in copies:
-        slot = everything.at[1 - head, source, half]
-        remote(slot, slot, twin_send.at[source, half], twin_recv.at[source, half],
-               twin).wait_recv()
-
-
-def third_kernel(n, own_ref, other_ref, resid_ref, out_ref, twin_in, send_buf, recv_buf,
-                 twin_send, twin_recv, ring_send, ring_recv):
-    frame, head = lax.axis_index("frame"), lax.axis_index("head")
-    place = ring_place(frame, n)
-    twin = {"head": 1 - head}
-    ends = [ring_frame((place + 1) % n, n), ring_frame((place + n - 1) % n, n)]
-    far = n // 2
-    greet([twin, {"frame": ends[0]}, {"frame": ends[1]}])
-    schedule = [
-        (step, way, half)
-        for step in range(1, far + 1)
-        for half in range(2)
-        for way in range(2)
-        if step > 1 or way == half
-    ]
-
-    def target(step, way):
+    gathers = ring_gather(lambda source, half: everything.at[head, source, half], place, n,
+                          ring_send, ring_recv, to_twin, up_blocks)
+
+    def frame_of(way, ahead):
+        return ring_frame((place + (ahead if way == 0 else n - ahead)) % n, n)
+
+    twins = {}
+
+    def produce(way, ahead):
+        q = frame_of(way, ahead)
+        blend = (
+            taps_ref[0:1] * hidden[q] + taps_ref[1:2] * hidden[q + 1]
+            + taps_ref[2:3] * hidden[q + 2]
+        ).astype(jnp.bfloat16)
+        mixed[q] = blend
+        product = against(blend, down_ref[1 - head]).astype(jnp.bfloat16)
+        for half in range(2):
+            theirs[q, half] = product[half * rows:(half + 1) * rows]
+            at = len(twins)
+            copy = remote(theirs.at[q, half], twin_in.at[q, half], sum_twin_send.at[at],
+                          sum_twin_recv.at[at], twin)
+            copy.start()
+            twins[way, ahead, half] = copy
+
+    def produce_step(step):
         ahead = far + 1 - step
-        return ring_frame((place + (ahead if way == 0 else n - ahead)) % n, n)
-
-    twins = {}
-    order = [(far, half) for half in range(2)]
-    order = []
-    for step, way, half in schedule:
-        key = (1 if step == 1 else way, far + 1 - step, half)
-        if key not in order:
-            order.append(key)
-    order += [(0, 0, 0), (0, 0, 1)]
-
-    def frame_of(key):
-        way, ahead, half = key
-        return ring_frame((place + (ahead if way == 0 else n - ahead)) % n, n)
-
-    for at, key in enumerate(order):
-        q = frame_of(key)
-        copy = remote(other_ref.at[q, key[2]], twin_in.at[q, key[2]], twin_send.at[at],
-                      twin_recv.at[at], twin)
-        copy.start()
-        twins[key] = copy
-
-    def term(key):
-        twins[key].wait()
-        q = frame_of(key)
-        return own_ref[q, key[2]] + twin_in[q, key[2]].astype(jnp.float32)
+        produce(1, ahead)
+        if 0 < ahead < far:
+            produce(0, ahead)
+
+    def terms(way, ahead):
+        q = frame_of(way, ahead)
+        own = against(mixed[q], down_ref[head])
+        out = []
+        for half in range(2):
+            twins[way, ahead, half].wait()
+            out.append(own[half * rows:(half + 1) * rows]
+                       + twin_in[q, half].astype(jnp.float32))
+        return out
 
     def arrival(step, way, half):
         slot = recv_buf.at[way, step - 1, half]
-        remote(slot, slot, ring_send.at[way, step, half], ring_recv.at[way, step, half],
+        remote(slot, slot, sum_send.at[way, step, half], sum_recv.at[way, step, half],
                {"frame": ends[way]}).wait_recv()
         return recv_buf[way, step - 1, half].astype(jnp.float32)
 
     started = []
-    for step, way, half in schedule:
-        key = (1 if step == 1 else way, far + 1 - step, half)
-        total = term(key)
+
+    def send_sum(step, way, half, total):
         if step > 2 or (step == 2 and way == half):
             total = total + arrival(step - 1, way, half)
         send_buf[way, step - 1, half] = total.astype(jnp.bfloat16)
         copy = remote(send_buf.at[way, step - 1, half], recv_buf.at[way, step - 1, half],
-                      ring_send.at[way, step, half], ring_recv.at[way, step, half],
+                      sum_send.at[way, step, half], sum_recv.at[way, step, half],
                       {"frame": ends[way]})
         copy.start()
         started.append(copy)
-    rows = out_ref.shape[0] // 2
+
+    produce_step(1)
+    produce_step(2)
+    for step in range(1, far + 1):
+        ahead = far + 1 - step
+        if step == 1:
+            held = terms(1, ahead)
+            send_sum(1, 0, 0, held[0])
+            send_sum(1, 1, 1, held[1])
+        else:
+            held = [terms(0, ahead), terms(1, ahead)]
+            for half in range(2):
+                for way in range(2):
+                    send_sum(step, way, half, held[way][half])
+        if step < far:
+            produce_step(step + 2)
+    held = terms(1, 0)
     for half in range(2):
-        total = term((0, 0, half))
+        total = held[half]
         for way in range(2):
             total = total + arrival(far, way, half)
-        block = resid_ref[half * rows:(half + 1) * rows].astype(jnp.float32)
+        block = resid[half * rows:(half + 1) * rows].astype(jnp.float32)
         out_ref[half * rows:(half + 1) * rows] = (block + total).astype(jnp.bfloat16)
-    for copy in started:
+    for copy in started + copies + gathers:
         copy.wait_send()
+
+
+def against(x, y):
+    return lax.dot_general(x, y, (((1,), (1,)), ((), ())), preferred_element_type=jnp.float32)
 
 
 VMEM = pl.BlockSpec(memory_space=pltpu.VMEM)
@@ -458,19 +493,18 @@
     up_rows, hidden = w_up.shape
     part = hidden // n
     out_cols = w_down.shape[1]
-    states, weights, proj = call(
+    states, weights, proj_t = call(
         functools.partial(first_kernel, n), 0,
         [
             jax.ShapeDtypeStruct((n,) + sent.shape, bf16),
             jax.ShapeDtypeStruct((2, n, up_rows, part), bf16),
-            jax.ShapeDtypeStruct((n, 2, out_cols // 2, w_out.shape[0]), bf16),
+            jax.ShapeDtypeStruct((n * out_cols, w_out.shape[0]), bf16),
         ],
-        [pltpu.VMEM((2, n, up_rows, part), bf16), dma((4,))] + ring
+        [pltpu.VMEM((n, 2, out_cols // 2, w_out.shape[0]), bf16),
+         pltpu.VMEM((2, n, up_rows, part), bf16), dma((4,))] + ring
         + [dma((2, far + 1)), dma((2, far + 1)), dma((n,)), dma((n,)), dma((2 * n,)), dma((2 * n,))],
         sent, w_up, w_down.T, w_out.T.reshape(2, out_cols // 2, w_out.shape[0]),
     )
-    up_all, down_all = weights[0], weights[1]
-    proj_t = proj.reshape(n * out_cols, w_out.shape[0])
     earlier = (jnp.arange(n) < frame).astype(f32)
     state = own_state + jnp.sum(
         states.astype(f32) * earlier[:, None, None, None], axis=0
@@ -485,58 +519,35 @@
     )
     gained = (attended * attn_gain).astype(bf16)
     width = stream.shape[1]
-    def against(x, y):
-        return lax.dot_general(x, y, (((1,), (1,)), ((), ())), preferred_element_type=f32)
-
     half_out = [
         against(gained, lax.dynamic_slice_in_dim(proj_t, at * width, width, 0))
         for at in (head, 1 - head)
     ]
     gain_here = lax.dynamic_slice_in_dim(ffn_gain, head * width, width, 0)[None]
-    everything, resid = call(
+    taps = lax.dynamic_slice_in_dim(conv_taps, frame * part, part, 1)
+    both_weights = weights.reshape(2, 2, width, part)
+    shape = (n, 2, tokens // 2, width)
+    link = (2, far, 2, tokens // 2, width)
+    return call(
         functools.partial(second_kernel, n, HEADS * HEAD_DIM, D), 1,
+        jax.ShapeDtypeStruct((tokens, width), bf16),
         [
-            jax.ShapeDtypeStruct((2, n, 2, tokens // 2, width), bf16),
-            jax.ShapeDtypeStruct((tokens, width), bf16),
-        ],
-        [
+            pltpu.VMEM((2,) + shape, bf16),
+            pltpu.VMEM((tokens, width), bf16),
             pltpu.VMEM((tokens, width), f32),
             pltpu.VMEM((tokens, 128), f32),
             pltpu.VMEM((tokens, 128), f32),
             pltpu.VMEM((tokens, 128), f32),
+            pltpu.VMEM((n + 2, tokens, part), f32),
+            pltpu.VMEM((n, tokens, part), bf16),
+            pltpu.VMEM(shape, bf16),
+            pltpu.VMEM(shape, bf16),
+            pltpu.VMEM(link, bf16),
+            pltpu.VMEM(link, bf16),
             dma((3,)), dma((3,)),
-        ] + ring + [dma((n, 2)), dma((n, 2))],
+        ] + ring + [dma((n, 2)), dma((n, 2)), dma((2 * n,)), dma((2 * n,))] + ring,
         half_out[0], half_out[1], squares, stream, gain_here,
-    )
-    ffn_in = everything.reshape(2, n * tokens, width)
-    up_full = up_all.reshape(2, width, part)
-    up_value = jnp.dot(ffn_in[0], up_full[0], preferred_element_type=f32) + jnp.dot(
-        ffn_in[1], up_full[1], preferred_element_type=f32
-    )
-    hidden_all = jax.nn.silu(up_value).astype(bf16).reshape(n * tokens // TPF, TPF, part)
-    padded = jnp.pad(hidden_all, ((1, 1), (0, 0), (0, 0))).astype(f32)
-    taps = lax.dynamic_slice_in_dim(conv_taps, frame * part, part, 1)
-    mixed = taps[0] * padded[:-2] + taps[1] * padded[1:-1] + taps[2] * padded[2:]
-    mixed = mixed.astype(bf16).reshape(n * tokens, part)
-
-    def down_half(at):
-        return against(
-            mixed, lax.dynamic_slice_in_dim(down_all, at * (n // 2), n // 2, 0).reshape(width, part)
-        )
-
-    own = down_half(head)
-    other = down_half(1 - head).astype(bf16)
-    shape = (n, 2, tokens // 2, width)
-    return call(
-        functools.partial(third_kernel, n), 2,
-        jax.ShapeDtypeStruct((tokens, width), bf16),
-        [
-            pltpu.VMEM(shape, bf16),
-            pltpu.VMEM((2, far, 2, tokens // 2, width), bf16),
-            pltpu.VMEM((2, far, 2, tokens // 2, width), bf16),
-            dma((2 * n,)), dma((2 * n,)),
-        ] + ring,
-        own.reshape(shape), other.reshape(shape), resid,
+        both_weights[0], both_weights[1], taps,
     )
 
 
@@ -563,6 +574,7 @@
             group_tokens <= hidden
             and heads == 2
             and mesh.shape["groups"] == 2
+            and group_tokens == frames * TPF
             and frames % 2 == 0
             and frames >= 4
             and hidden % (heads * frames) == 0

time: 203 us -> 172 us (0.85)
  other arithmetic: 12.1 us -> 2.39 us
  local copies, waits for them, and re-layouts: 22.7 us -> 13.4 us
  matrix products: 12.9 us -> 7.34 us
  Pallas kernels: 154 us -> 149 us
    dot_general x6 -> x2, matrix products: 11.2 us -> 3.95 us  [against(): lax.dot_general(x, y, (((1,), (1,)), ((), ())), preferred_element_type=jn...]
    pallas_call x3 -> x2, Pallas kernels: 154 us -> 149 us  [call(): pl.pallas_call(kernel, out_shape=outs, in_specs=[VMEM] * len(args), out_s...]
    convert_element_type x2 -> x0, other arithmetic: 5.2 us -> none  [the longest x1 3.84 us: token_body(): mixed = mixed.astype(bf16).reshape(n * tokens, part)]
    reshape x2 -> x0, local copies, waits for them, and re-layouts: 4.69 us -> none  [the longest x1 4.66 us: token_body(): proj_t = proj.reshape(n * out_cols, w_out.shape[0])]
    convert_element_type x2 -> x0, local copies, waits for them, and re-layouts: 4.26 us -> none  [the longest x1 2.98 us: token_body(): other = down_half(1 - head).astype(bf16)]
    unnamed x1 -> x0, other arithmetic: 3.17 us -> none
    slice x4 -> x1, local copies, waits for them, and re-layouts: 4.05 us -> 1.75 us  [token_body(): both_weights[1]]
    unnamed x23 -> x22, local copies, waits for them, and re-layouts: 6.41 us -> 6.7 us
where the time goes in v3:
time: 172 us
  Pallas kernels  149 us (87%)
  local copies, waits for them, and re-layouts  13.4 us (8%)
  matrix products  7.34 us (4%)
  other arithmetic  2.39 us (1%)
    pallas_call x2, Pallas kernels, call(): pl.pallas_call(kernel, out_shape=outs, in_specs=[VMEM] * len(args), out_s...  149 us
    unnamed x22, local copies, waits for them, and re-layouts  6.7 us
    dot_general x2, matrix products, against(): lax.dot_general(x, y, (((1,), (1,)), ((), ())), preferred_element_type=jn...  3.95 us

profile of v3, /device:TPU:0, one launch (start us, length us, event | category | flops | bytes accessed | tf_op | source)
XLA Modules:
  0.0 171.9 jit_solution(6090754009836054419)
XLA Ops:
  0.0 0.0 copy-start
  0.0 0.0 copy-start.5
  0.0 0.0 copy-start.4
  0.0 1.2 copy.15
  1.2 0.9 broadcast_maximum_fusion.1
  2.2 2.0 %fusion.14 = (bf16[5,112,128]{2,1,0:T(8,128)(2,1)}, f32[5,112,128]{2,1,0:T(8,128)}) fusion(bf16[128,5,112]{0,2,1:T(8,128)(2,1)S(1)} %bitcast.27, bf16[128,5,16]{2,0,1:T(8,128)(2,1)} %constant.45.clone.1, bf16[128,5,112]{2,0,1:T(8,128)(2,1)S(1)} %copy.15), kind=kOutput, calls=%fused_computation.25 | convolution fusion | flops 18749440 | bytes 737280 | tf_op jit(solution)/shard_map/thb,thc->hbc/dot_general | solution.py:490
  4.1 1.0 reshape.64.proj_ref
  5.2 0.0 copy-done.5
  5.2 0.0 copy-done.4
  5.2 0.0 copy-start.6
  5.2 0.9 copy-done.6
  6.1 78.5 %shard_map.100 = (bf16[8,2,280,128]{3,2,1,0:T(8,128)(2,1)S(1)}, bf16[2,8,280,210]{3,2,1,0:T(8,128)(2,1)S(1)}, bf16[2240,560]{1,0:T(8,128)(2,1)}) custom-call(bf16[2,280,128]{2,1,0:T(8,128)(2,1)S(1)} %bitcast.25, bf16[280,1680]{1,0:T(8,128)(2,1)S(1)} %copy-done.4, bf16[280,1680]{1,0:T(8,128)(2,1)S(1)} %bitcast.24, bf16[2,140,560]{2,1,0:T(8,128)(2,1)S(1)} %reshape.64.proj_ref), custom_call_target="tpu_custom_call" | custom-call | tf_op jit(solution)/shard_map/pallas_call | solution.py:458
  84.6 0.0 copy-start.1
  84.6 1.4 copy-done.1
  86.0 0.0 copy-start.9
  86.0 0.3 multiply_reduce_fusion
  86.3 0.9 broadcast_maximum_fusion
  87.3 1.4 convolution_bitcast_fusion
  88.7 0.1 multiply_reduce_fusion.1
  88.8 0.0 copy-done.9
  88.8 0.1 fusion.4
  89.0 0.0 copy-start.8
  89.0 2.0 %fusion.2.own_ref = f32[128,1120]{1,0:T(8,128)S(1)} fusion(bf16[128,560]{0,1:T(8,128)(2,1)S(1)} %fusion.4, bf16[2240,560]{1,0:T(8,128)(2,1)} %get-tuple-element.21, s32[]{:T(128)S(6)} %select_n.10), kind=kOutput, calls=%fused_computation.3 | convolution fusion | flops 160563200 | bytes 2150404 | tf_op jit(solution)/shard_map/dot_general | solution.py:451
  91.0 2.0 %fusion.other_ref = f32[128,1120]{1,0:T(8,128)S(1)} fusion(bf16[128,560]{0,1:T(8,128)(2,1)S(1)} %fusion.4, bf16[2240,560]{1,0:T(8,128)(2,1)} %get-tuple-element.21, s32[]{:T(128)S(6)} %select_n.11), kind=kOutput, calls=%fused_computation.1 | convolution fusion | flops 160563200 | bytes 2150404 | tf_op jit(solution)/shard_map/dot_general | solution.py:451
  93.0 0.7 broadcast_in_dim.4.sq_ref
  93.7 0.0 copy-done.8
  93.7 0.1 dynamic_slice.14
  93.8 0.0 copy-done
  93.8 0.1 constant_dynamic-slice_fusion.taps_ref
  93.8 1.8 %fusion.13 = (bf16[1,8,280,210]{3,2,1,0:T(8,128)(2,1)S(1)}, bf16[1,8,280,210]{3,2,1,0:T(8,128)(2,1)S(1)}) fusion(bf16[2,8,280,210]{3,2,1,0:T(8,128)(2,1)} %copy-done.1), kind=kLoop, calls=%fused_computation.24 | loop fusion | bytes 3763200 | tf_op jit(solution)/shard_map/slice | solution.py:550
  95.6 1.9 %copy.18.stream_ref = bf16[128,1120]{1,0:T(8,128)(2,1)} copy(bf16[128,1120]{0,1:T(8,128)(2,1)} %param.12) | data formatting | bytes 573440 | tf_op args[0]
  97.4 0.0 copy-start.3
  97.4 1.0 copy-done.3
  98.4 0.0 copy-start.7
  98.4 0.8 copy-done.7
  99.2 70.1 %shard_map.101 = bf16[128,1120]{1,0:T(8,128)(2,1)S(1)} custom-call(f32[128,1120]{1,0:T(8,128)S(1)} %fusion.2.own_ref, f32[128,1120]{1,0:T(8,128)S(1)} %fusion.other_ref, f32[128,128]{1,0:T(8,128)S(1)} %copy-done.7, bf16[128,1120]{1,0:T(8,128)(2,1)S(1)} %copy-done.3, f32[1,1120]{1,0:T(1,128)S(1)} %broadcast_in_dim.5.gain_ref, ...), custom_call_target="tpu_custom_call" | custom-call | tf_op jit(solution)/shard_map/pallas_call | solution.py:458
  169.3 0.0 copy-start.2
  169.3 0.7 copy-done.2
  170.0 1.8 %copy.19 = bf16[128,1120]{0,1:T(8,128)(2,1)} copy(bf16[128,1120]{1,0:T(8,128)(2,1)} %copy-done.2) | data formatting | bytes 573440 | tf_op jit(solution)/shard_map/pallas_call | solution.py:458
  (4 shorter events, 0.0 us)
Async XLA Ops:
  0.0 93.8 %copy-start = (f32[3,1680]{1,0:T(4,128)S(1)}, f32[3,1680]{1,0:T(4,128)}, u32[]{:S(2)}) copy-start(f32[3,1680]{1,0:T(4,128)} %param.20) | copy-start | bytes 60484
  0.0 5.2 %copy-start.5 = (bf16[1680,280]{0,1:T(8,128)(2,1)S(1)}, bf16[1680,280]{0,1:T(8,128)(2,1)}, u32[]{:S(2)}) copy-start(bf16[1680,280]{0,1:T(8,128)(2,1)} %param.21) | copy-start | bytes 2822404
  0.0 5.2 %copy-start.4 = (bf16[280,1680]{1,0:T(8,128)(2,1)S(1)}, bf16[280,1680]{1,0:T(8,128)(2,1)}, u32[]{:S(2)}) copy-start(bf16[280,1680]{1,0:T(8,128)(2,1)} %up_ref.1) | copy-start | bytes 2822404
  5.2 0.9 copy-start.6
  84.6 1.4 copy-start.1
  86.0 2.8 %copy-start.9 = (f32[560]{0:T(1024)S(1)}, f32[560]{0:T(1024)}, u32[]{:S(2)}) copy-start(f32[560]{0:T(1024)} %param.16) | copy-start | bytes 6724
  89.0 4.7 %copy-start.8 = (f32[2240]{0:T(1024)S(1)}, f32[2240]{0:T(1024)}, u32[]{:S(2)}) copy-start(f32[2240]{0:T(1024)} %param.18) | copy-start | bytes 26884
  97.4 1.0 copy-start.3
  98.4 0.8 copy-start.7
  169.3 0.7 copy-start.2

commit v4 on v3

--- a/solution.py
+++ b/solution.py
@@ -191,8 +191,8 @@
     return started
 
 
-def first_kernel(n, state_ref, up_ref, down_ref, proj_ref, states, weights, merged, proj,
-                 blocks, here,
+def first_kernel(n, state_ref, total_ref, query_ref, gain_ref, up_ref, down_ref, proj_ref,
+                 weights, own_out, other_out, sq_out, states, merged, proj, blocks, here,
                  state_send, state_recv, proj_send, proj_recv, all_send, all_recv,
                  over_send, over_recv):
     frame, group = lax.axis_index("frame"), lax.axis_index("groups")
@@ -292,8 +292,29 @@
     count = proj.shape[2]
     for at in range(n):
         for half in range(2):
-            first_row = (2 * at + half) * count
-            merged[first_row:first_row + count] = proj[at, half]
+            side, first_row = at // far, (2 * (at % far) + half) * count
+            merged[side, first_row:first_row + count] = proj[at, half]
+    heads_here = query_ref.shape[0]
+    before = jnp.zeros(states.shape[1:], jnp.float32)
+    for at in range(n):
+        seen = jnp.where(at < frame, 1.0, 0.0)
+        before = before + states[at].astype(jnp.float32) * seen
+    before = before.reshape(-1, before.shape[-1])
+    depth = query_ref.shape[1]
+    squares, pieces = 0.0, []
+    for at in range(heads_here):
+        query = query_ref[at].astype(jnp.float32).T
+        state = total_ref[at] + before[at * depth:(at + 1) * depth]
+        both = jnp.dot(query, state, precision=lax.Precision.HIGHEST,
+                       preferred_element_type=jnp.float32)
+        attended = both[:, :depth] / (both[:, depth:depth + 1] + 1e-06)
+        squares = squares + jnp.sum(attended * attended, axis=1, keepdims=True)
+        pieces.append(attended)
+    sq_out[...] = jnp.broadcast_to(squares, sq_out.shape)
+    gained = (jnp.concatenate(pieces, axis=1) * gain_ref[...]).astype(jnp.bfloat16)
+    head = lax.axis_index("head")
+    own_out[...] = against(gained, merged[head])
+    other_out[...] = against(gained, merged[1 - head])
     for k in ways:
         swapped_in(weights.at[1 - group, (frame + n - k) % n], 2 * far + k)
     for copy in swapped:
@@ -303,7 +324,7 @@
 
 
 def second_kernel(n, features, width, own_ref, other_ref, sq_ref, stream_ref, gain_ref,
-                  up_ref, down_ref, taps_ref, out_ref,
+                  weights_ref, taps_ref, out_ref,
                   everything, resid, arrived, sq_in, sq_mine, sq_two, hidden, mixed, theirs,
                   twin_in, send_buf, recv_buf,
                   pair_send, pair_recv, ring_send, ring_recv, twin_send, twin_recv,
@@ -356,7 +377,7 @@
                 block = jnp.concatenate(
                     [everything[at, source, 0], everything[at, source, 1]], axis=0
                 )
-                term = jnp.dot(block, up_ref[at], preferred_element_type=jnp.float32)
+                term = jnp.dot(block, weights_ref[0, at], preferred_element_type=jnp.float32)
                 total = term if total is None else total + term
             act = total / (1.0 + jnp.exp(-total))
             hidden[source + 1] = act.astype(jnp.bfloat16).astype(jnp.float32)
@@ -378,7 +399,7 @@
             + taps_ref[2:3] * hidden[q + 2]
         ).astype(jnp.bfloat16)
         mixed[q] = blend
-        product = against(blend, down_ref[1 - head]).astype(jnp.bfloat16)
+        product = against(blend, weights_ref[1, 1 - head]).astype(jnp.bfloat16)
         for half in range(2):
             theirs[q, half] = product[half * rows:(half + 1) * rows]
             at = len(twins)
@@ -395,7 +416,7 @@
 
     def terms(way, ahead):
         q = frame_of(way, ahead)
-        own = against(mixed[q], down_ref[head])
+        own = against(mixed[q], weights_ref[1, head])
         out = []
         for half in range(2):
             twins[way, ahead, half].wait()
@@ -483,7 +504,6 @@
         return x.reshape(tokens, heads_here, HEAD_DIM)
 
     pad = 128
-    qpos = split(jnp.maximum(queries, 0))
     kpos = split(jnp.maximum(key_rows, 0))
     ones = jnp.zeros((tokens, heads_here, pad - HEAD_DIM), bf16).at[:, :, 0].set(1)
     values = jnp.concatenate([split(value_rows), ones], axis=2)
@@ -493,36 +513,24 @@
     up_rows, hidden = w_up.shape
     part = hidden // n
     out_cols = w_down.shape[1]
-    states, weights, proj_t = call(
+    width = stream.shape[1]
+    query_t = jnp.maximum(queries, 0).T.reshape(heads_here, HEAD_DIM, tokens)
+    weights, half_own, half_other, squares = call(
         functools.partial(first_kernel, n), 0,
         [
-            jax.ShapeDtypeStruct((n,) + sent.shape, bf16),
             jax.ShapeDtypeStruct((2, n, up_rows, part), bf16),
-            jax.ShapeDtypeStruct((n * out_cols, w_out.shape[0]), bf16),
+            jax.ShapeDtypeStruct((tokens, width), f32),
+            jax.ShapeDtypeStruct((tokens, width), f32),
+            jax.ShapeDtypeStruct((tokens, 128), f32),
         ],
-        [pltpu.VMEM((n, 2, out_cols // 2, w_out.shape[0]), bf16),
+        [pltpu.VMEM((n,) + sent.shape, bf16),
+         pltpu.VMEM((2, width, w_out.shape[0]), bf16),
+         pltpu.VMEM((n, 2, out_cols // 2, w_out.shape[0]), bf16),
          pltpu.VMEM((2, n, up_rows, part), bf16), dma((4,))] + ring
         + [dma((2, far + 1)), dma((2, far + 1)), dma((n,)), dma((n,)), dma((2 * n,)), dma((2 * n,))],
-        sent, w_up, w_down.T, w_out.T.reshape(2, out_cols // 2, w_out.shape[0]),
-    )
-    earlier = (jnp.arange(n) < frame).astype(f32)
-    state = own_state + jnp.sum(
-        states.astype(f32) * earlier[:, None, None, None], axis=0
-    ).reshape(own_state.shape)
-    both = jnp.einsum(
-        "thb,hbc->thc", qpos.astype(f32), state, precision=lax.Precision.HIGHEST
-    )
-    attended = both[:, :, :HEAD_DIM] / (both[:, :, HEAD_DIM:HEAD_DIM + 1] + 1e-06)
-    attended = attended.reshape(tokens, heads_here * HEAD_DIM)
-    squares = jnp.broadcast_to(
-        jnp.sum(attended * attended, axis=1, keepdims=True), (tokens, 128)
-    )
-    gained = (attended * attn_gain).astype(bf16)
-    width = stream.shape[1]
-    half_out = [
-        against(gained, lax.dynamic_slice_in_dim(proj_t, at * width, width, 0))
-        for at in (head, 1 - head)
-    ]
+        sent, own_state, query_t, attn_gain[None], w_up, w_down.T,
+        w_out.T.reshape(2, out_cols // 2, w_out.shape[0]),
+    )
     gain_here = lax.dynamic_slice_in_dim(ffn_gain, head * width, width, 0)[None]
     taps = lax.dynamic_slice_in_dim(conv_taps, frame * part, part, 1)
     both_weights = weights.reshape(2, 2, width, part)
@@ -546,8 +554,8 @@
             pltpu.VMEM(link, bf16),
             dma((3,)), dma((3,)),
         ] + ring + [dma((n, 2)), dma((n, 2)), dma((2 * n,)), dma((2 * n,))] + ring,
-        half_out[0], half_out[1], squares, stream, gain_here,
-        both_weights[0], both_weights[1], taps,
+        half_own, half_other, squares, stream, gain_here,
+        both_weights, taps,
     )
 
 

time: 172 us -> 164 us (0.953)
  matrix products: 7.34 us -> 1.21 us
  local copies, waits for them, and re-layouts: 13.4 us -> 9.44 us
    dot_general x3 -> x0, matrix products: 5.38 us -> none  [the longest x2 3.95 us: against(): lax.dot_general(x, y, (((1,), (1,)), ((), ())), preferred_element_type=jn...]
    slice x1 -> x0, local copies, waits for them, and re-layouts: 1.75 us -> none  [token_body(): both_weights[1]]
    unnamed x22 -> x17, local copies, waits for them, and re-layouts: 6.7 us -> 5.59 us
where the time goes in v4:
time: 164 us
  Pallas kernels  150 us (91%)
  local copies, waits for them, and re-layouts  9.44 us (6%)
  other arithmetic  2.65 us (2%)
    pallas_call x2, Pallas kernels, call(): pl.pallas_call(kernel, out_shape=outs, in_specs=[VMEM] * len(args), out_s...  150 us
    unnamed x17, local copies, waits for them, and re-layouts  5.59 us

profile of v4, /device:TPU:0, one launch (start us, length us, event | category | flops | bytes accessed | tf_op | source)
XLA Modules:
  0.0 163.6 jit_solution(17609209318536733870)
XLA Ops:
  0.0 0.0 copy-start
  0.0 0.0 copy-start.2
  0.0 0.0 copy-start.3
  0.0 1.1 broadcast_maximum_fusion.1
  1.1 1.1 copy.13
  2.1 1.2 fusion.5
  3.4 0.0 copy-start.7
  3.4 1.6 broadcast_maximum_fusion
  5.0 0.7 broadcast_in_dim.8.gain_ref
  5.6 1.0 reshape.50.proj_ref
  6.7 0.0 copy-done.2
  6.7 0.0 copy-done.3
  6.7 0.0 copy-start.6
  6.7 0.9 copy-done.6
  7.6 80.2 %shard_map.100 = (bf16[2,8,280,210]{3,2,1,0:T(8,128)(2,1)}, f32[128,1120]{1,0:T(8,128)S(1)}, f32[128,1120]{1,0:T(8,128)S(1)}, f32[128,128]{1,0:T(8,128)S(1)}) custom-call(bf16[2,280,128]{2,1,0:T(8,128)(2,1)S(1)} %bitcast.12, f32[5,112,128]{2,1,0:T(8,128)S(1)} %get-tuple-element.26.total_ref, bf16[5,112,128]{2,1,0:T(8,128)(2,1)S(1)} %bitcast.13, ...), custom_call_target="tpu_custom_call" | custom-call | tf_op jit(solution)/shard_map/pallas_call | solution.py:479
  87.8 0.0 copy-start.4
  87.8 0.8 copy-done.4
  88.6 1.2 copy.14.stream_ref
  89.8 0.0 copy-done.7
  89.8 0.1 dynamic_slice.6
  89.9 0.0 copy-done
  89.9 0.1 constant_dynamic-slice_fusion.taps_ref
  90.0 0.0 copy-start.1
  90.0 1.6 %copy-done.1 = bf16[2,8,280,210]{3,2,1,0:T(8,128)(2,1)S(1)} copy-done((bf16[2,8,280,210]{3,2,1,0:T(8,128)(2,1)S(1)}, bf16[2,8,280,210]{3,2,1,0:T(8,128)(2,1)}, u32[]{:S(2)}) %copy-start.1) | copy-done | bytes 1881624
  91.6 0.0 copy-start.5
  91.6 1.1 copy-done.5
  92.7 70.0 %shard_map.101 = bf16[128,1120]{1,0:T(8,128)(2,1)S(1)} custom-call(f32[128,1120]{1,0:T(8,128)S(1)} %get-tuple-element.21.own_ref, f32[128,1120]{1,0:T(8,128)S(1)} %copy-done.5, f32[128,128]{1,0:T(8,128)S(1)} %get-tuple-element.23.sq_ref, bf16[128,1120]{1,0:T(8,128)(2,1)S(1)} %copy.14.stream_ref, f32[1,1120]{1,0:T(1,128)S(1)} %broadcast_in_dim.9.gain_ref, ...), custom_call_target="tpu_custom_call" | custom-call | tf_op jit(solution)/shard_map/pallas_call | solution.py:479
  162.7 0.9 copy.15
  (1 shorter events, 0.0 us)
Async XLA Ops:
  0.0 89.9 %copy-start = (f32[3,1680]{1,0:T(4,128)S(1)}, f32[3,1680]{1,0:T(4,128)}, u32[]{:S(2)}) copy-start(f32[3,1680]{1,0:T(4,128)} %param.20) | copy-start | bytes 60484
  0.0 6.7 %copy-start.2 = (bf16[280,1680]{1,0:T(8,128)(2,1)S(1)}, bf16[280,1680]{1,0:T(8,128)(2,1)}, u32[]{:S(2)}) copy-start(bf16[280,1680]{1,0:T(8,128)(2,1)} %up_ref.1) | copy-start | bytes 2822404
  0.0 6.7 %copy-start.3 = (bf16[1680,280]{0,1:T(8,128)(2,1)S(1)}, bf16[1680,280]{0,1:T(8,128)(2,1)}, u32[]{:S(2)}) copy-start(bf16[1680,280]{0,1:T(8,128)(2,1)} %param.21) | copy-start | bytes 2822404
  3.4 86.4 %copy-start.7 = (f32[2240]{0:T(1024)S(1)}, f32[2240]{0:T(1024)}, u32[]{:S(2)}) copy-start(f32[2240]{0:T(1024)} %param.18) | copy-start | bytes 26884
  6.7 0.9 copy-start.6
  87.8 0.8 copy-start.4
  90.0 1.6 %copy-start.1 = (bf16[2,8,280,210]{3,2,1,0:T(8,128)(2,1)S(1)}, bf16[2,8,280,210]{3,2,1,0:T(8,128)(2,1)}, u32[]{:S(2)}) copy-start(bf16[2,8,280,210]{3,2,1,0:T(8,128)(2,1)} %get-tuple-element.24) | copy-start | bytes 5644804
  91.6 1.1 copy-start.5

commit v5 on v4

--- a/solution.py
+++ b/solution.py
@@ -215,7 +215,8 @@
             pltpu.make_async_copy(blocks.at[at, frame], weights.at[at, frame], here.at[2 + at])
         )
         local[-1].start()
-    greet([{"frame": (frame + k) % n} for k in range(1, n)] + [over])
+    greet([{"frame": (frame + k) % n} for k in range(1, n)]
+          + [over, {"head": 1 - lax.axis_index("head")}])
     local[0].wait()
     local[1].wait()
 
@@ -279,9 +280,6 @@
         for way in range(2):
             last = far if way == half else far - 1
             state_copy(last, way, half, origin(last, way)).wait_recv()
-    for copy in ring + pushed:
-        copy.wait_send()
-
     def swapped_in(slot, at):
         remote(slot, slot, over_send.at[at], over_recv.at[at], over).wait_recv()
 
@@ -315,15 +313,17 @@
     head = lax.axis_index("head")
     own_out[...] = against(gained, merged[head])
     other_out[...] = against(gained, merged[1 - head])
-    for k in ways:
-        swapped_in(weights.at[1 - group, (frame + n - k) % n], 2 * far + k)
-    for copy in swapped:
-        copy.wait_send()
-    local[2].wait()
-    local[3].wait()
-
-
-def second_kernel(n, features, width, own_ref, other_ref, sq_ref, stream_ref, gain_ref,
+
+    def ready():
+        for k in ways:
+            swapped_in(weights.at[1 - group, (frame + n - k) % n], 2 * far + k)
+        local[2].wait()
+        local[3].wait()
+
+    return ready, ring + pushed + swapped
+
+
+def second_kernel(n, features, width, ready, own_ref, other_ref, sq_ref, stream_ref, gain_ref,
                   weights_ref, taps_ref, out_ref,
                   everything, resid, arrived, sq_in, sq_mine, sq_two, hidden, mixed, theirs,
                   twin_in, send_buf, recv_buf,
@@ -337,7 +337,6 @@
     rows = stream_ref.shape[0] // 2
     hidden[0] = jnp.zeros_like(hidden[0])
     hidden[n + 1] = jnp.zeros_like(hidden[0])
-    greet([twin, {"frame": ends[0]}, {"frame": ends[1]}])
     first = remote(other_ref, arrived, pair_send.at[0], pair_recv.at[0], twin)
     second = remote(sq_ref, sq_in, pair_send.at[1], pair_recv.at[1], twin)
     second.start()
@@ -366,8 +365,20 @@
         copy.start()
         copies.append(copy)
 
+    waiting = []
+
+    def weights_of(which, side):
+        return jnp.concatenate(
+            [weights_ref[which, side * far + at] for at in range(far)], axis=0
+        )
+
     def up_blocks(sources):
-        for source in sources:
+        waiting.extend(sources)
+        if len(waiting) < n - 1:
+            return
+        if len(waiting) == n - 1:
+            ready()
+        for source in waiting if len(waiting) == n - 1 else sources:
             for half in range(2):
                 slot = everything.at[1 - head, source, half]
                 remote(slot, slot, twin_send.at[source, half], twin_recv.at[source, half],
@@ -377,7 +388,7 @@
                 block = jnp.concatenate(
                     [everything[at, source, 0], everything[at, source, 1]], axis=0
                 )
-                term = jnp.dot(block, weights_ref[0, at], preferred_element_type=jnp.float32)
+                term = jnp.dot(block, weights_of(0, at), preferred_element_type=jnp.float32)
                 total = term if total is None else total + term
             act = total / (1.0 + jnp.exp(-total))
             hidden[source + 1] = act.astype(jnp.bfloat16).astype(jnp.float32)
@@ -399,7 +410,7 @@
             + taps_ref[2:3] * hidden[q + 2]
         ).astype(jnp.bfloat16)
         mixed[q] = blend
-        product = against(blend, weights_ref[1, 1 - head]).astype(jnp.bfloat16)
+        product = against(blend, weights_of(1, 1 - head)).astype(jnp.bfloat16)
         for half in range(2):
             theirs[q, half] = product[half * rows:(half + 1) * rows]
             at = len(twins)
@@ -416,7 +427,7 @@
 
     def terms(way, ahead):
         q = frame_of(way, ahead)
-        own = against(mixed[q], weights_ref[1, head])
+        own = against(mixed[q], weights_of(1, head))
         out = []
         for half in range(2):
             twins[way, ahead, half].wait()
@@ -472,6 +483,21 @@
     return lax.dot_general(x, y, (((1,), (1,)), ((), ())), preferred_element_type=jnp.float32)
 
 
+def whole_kernel(n, features, width, state_ref, total_ref, query_ref, gain_ref, up_ref, down_ref,
+                 proj_ref, stream_ref, ffn_gain_ref, taps_ref, out_ref,
+                 weights, own, other, squares, *scratch):
+    ready, sent = first_kernel(
+        n, state_ref, total_ref, query_ref, gain_ref, up_ref, down_ref, proj_ref,
+        weights, own, other, squares, *scratch[:13],
+    )
+    second_kernel(
+        n, features, width, ready, own, other, squares, stream_ref, ffn_gain_ref,
+        weights, taps_ref, out_ref, *scratch[13:],
+    )
+    for copy in sent:
+        copy.wait_send()
+
+
 VMEM = pl.BlockSpec(memory_space=pltpu.VMEM)
 
 
@@ -515,31 +541,25 @@
     out_cols = w_down.shape[1]
     width = stream.shape[1]
     query_t = jnp.maximum(queries, 0).T.reshape(heads_here, HEAD_DIM, tokens)
-    weights, half_own, half_other, squares = call(
-        functools.partial(first_kernel, n), 0,
-        [
-            jax.ShapeDtypeStruct((2, n, up_rows, part), bf16),
-            jax.ShapeDtypeStruct((tokens, width), f32),
-            jax.ShapeDtypeStruct((tokens, width), f32),
-            jax.ShapeDtypeStruct((tokens, 128), f32),
-        ],
-        [pltpu.VMEM((n,) + sent.shape, bf16),
-         pltpu.VMEM((2, width, w_out.shape[0]), bf16),
-         pltpu.VMEM((n, 2, out_cols // 2, w_out.shape[0]), bf16),
-         pltpu.VMEM((2, n, up_rows, part), bf16), dma((4,))] + ring
-        + [dma((2, far + 1)), dma((2, far + 1)), dma((n,)), dma((n,)), dma((2 * n,)), dma((2 * n,))],
-        sent, own_state, query_t, attn_gain[None], w_up, w_down.T,
-        w_out.T.reshape(2, out_cols // 2, w_out.shape[0]),
-    )
     gain_here = lax.dynamic_slice_in_dim(ffn_gain, head * width, width, 0)[None]
     taps = lax.dynamic_slice_in_dim(conv_taps, frame * part, part, 1)
-    both_weights = weights.reshape(2, 2, width, part)
     shape = (n, 2, tokens // 2, width)
     link = (2, far, 2, tokens // 2, width)
     return call(
-        functools.partial(second_kernel, n, HEADS * HEAD_DIM, D), 1,
+        functools.partial(whole_kernel, n, HEADS * HEAD_DIM, D), 0,
         jax.ShapeDtypeStruct((tokens, width), bf16),
         [
+            pltpu.VMEM((2, n, up_rows, part), bf16),
+            pltpu.VMEM((tokens, width), f32),
+            pltpu.VMEM((tokens, width), f32),
+            pltpu.VMEM((tokens, 128), f32),
+            pltpu.VMEM((n,) + sent.shape, bf16),
+            pltpu.VMEM((2, width, w_out.shape[0]), bf16),
+            pltpu.VMEM((n, 2, out_cols // 2, w_out.shape[0]), bf16),
+            pltpu.VMEM((2, n, up_rows, part), bf16),
+            dma((4,)),
+        ] + ring + [
+            dma((2, far + 1)), dma((2, far + 1)), dma((n,)), dma((n,)), dma((2 * n,)), dma((2 * n,)),
             pltpu.VMEM((2,) + shape, bf16),
             pltpu.VMEM((tokens, width), bf16),
             pltpu.VMEM((tokens, width), f32),
@@ -554,8 +574,8 @@
             pltpu.VMEM(link, bf16),
             dma((3,)), dma((3,)),
         ] + ring + [dma((n, 2)), dma((n, 2)), dma((2 * n,)), dma((2 * n,))] + ring,
-        half_own, half_other, squares, stream, gain_here,
-        both_weights, taps,
+        sent, own_state, query_t, attn_gain[None], w_up, w_down.T,
+        w_out.T.reshape(2, out_cols // 2, w_out.shape[0]), stream, gain_here, taps,
     )
 
 

time: 164 us -> 155 us (0.945)
  local copies, waits for them, and re-layouts: 9.44 us -> 3.17 us
  Pallas kernels: 150 us -> 148 us
    unnamed x17 -> x21, local copies, waits for them, and re-layouts: 5.59 us -> 1.9 us
    pallas_call x2 -> x1, Pallas kernels: 150 us -> 148 us  [call(): pl.pallas_call(kernel, out_shape=outs, in_specs=[VMEM] * len(args), out_s...]
where the time goes in v5:
time: 155 us
  Pallas kernels  148 us (95%)
  local copies, waits for them, and re-layouts  3.17 us (2%)
  other arithmetic  1.64 us (1%)
    pallas_call x1, Pallas kernels, call(): pl.pallas_call(kernel, out_shape=outs, in_specs=[VMEM] * len(args), out_s...  148 us

profile of v5, /device:TPU:0, one launch (start us, length us, event | category | flops | bytes accessed | tf_op | source)
XLA Modules:
  0.0 154.5 jit_solution(13137263010859757432)
XLA Ops:
  0.0 0.0 copy-start
  0.0 0.0 copy-start.9
  0.0 0.0 copy-start.8
  0.0 0.7 copy-done.9
  0.7 0.1 copy-done
  0.8 0.1 constant_dynamic-slice_fusion.taps_ref
  0.8 0.0 copy-done.8
  0.8 0.1 dynamic_slice.6
  0.9 0.0 copy-start.6
  0.9 0.0 copy-start.7
  0.9 1.6 %broadcast_maximum_fusion = bf16[128,560]{0,1:T(8,128)(2,1)} fusion(bf16[128,560]{0,1:T(8,128)(2,1)} %param.13), kind=kLoop, calls=%fused_computation.4 | loop fusion | flops 71680 | bytes 286720 | tf_op jit(solution)/shard_map/max | solution.py:543
  2.6 0.0 copy-done.6
  2.6 0.0 copy-start.5
  2.6 0.0 copy-done.7
  2.6 0.0 copy-start.4
  2.6 0.2 copy.13
  2.8 0.0 copy-start.1
  2.8 0.0 copy-start.2
  2.8 1.3 fusion.5
  4.1 0.0 copy-done.5
  4.2 0.2 copy.14.stream_ref
  4.4 0.0 copy-done.4
  4.4 0.1 reshape.47.proj_ref
  4.4 0.0 copy-done.1
  4.5 0.0 copy-done.2
  4.5 0.0 copy-start.3
  4.5 0.9 copy-done.3
  5.4 148.3 %shard_map.100 = bf16[128,1120]{1,0:T(8,128)(2,1)S(1)} custom-call(bf16[2,280,128]{2,1,0:T(8,128)(2,1)S(1)} %bitcast.10, f32[5,112,128]{2,1,0:T(8,128)S(1)} %get-tuple-element.18.total_ref, bf16[5,112,128]{2,1,0:T(8,128)(2,1)S(1)} %bitcast.11, f32[1,560]{1,0:T(1,128)S(1)} %broadcast_in_dim.8.gain_ref, bf16[280,1680]{1,0:T(8,128)(2,1)S(1)} %copy-done.1, ...), custom_call_target="tpu_custom_call" | custom-call | tf_op jit(solution)/shard_map/pallas_call | solution.py:505
  153.7 0.9 copy.15
  (3 shorter events, 0.0 us)
Async XLA Ops:
  0.0 0.8 copy-start
  0.0 0.7 copy-start.9
  0.0 0.8 copy-start.8
  0.9 1.6 %copy-start.6 = (bf16[128,560]{0,1:T(8,128)(2,1)S(1)}, bf16[128,560]{0,1:T(8,128)(2,1)}, u32[]{:S(2)}) copy-start(bf16[128,560]{0,1:T(8,128)(2,1)} %param.14) | copy-start | bytes 430084
  0.9 1.7 %copy-start.7 = (bf16[128,560]{0,1:T(8,128)(2,1)S(1)}, bf16[128,560]{0,1:T(8,128)(2,1)}, u32[]{:S(2)}) copy-start(bf16[128,560]{0,1:T(8,128)(2,1)} %param.15) | copy-start | bytes 430084
  2.6 1.6 %copy-start.5 = (bf16[128,1120]{0,1:T(8,128)(2,1)S(1)}, bf16[128,1120]{0,1:T(8,128)(2,1)}, u32[]{:S(2)}) copy-start(bf16[128,1120]{0,1:T(8,128)(2,1)} %param.12) | copy-start | bytes 860164
  2.6 1.8 %copy-start.4 = (bf16[560,280]{0,1:T(8,128)(2,1)S(1)}, bf16[560,280]{0,1:T(8,128)(2,1)}, u32[]{:S(2)}) copy-start(bf16[560,280]{0,1:T(8,128)(2,1)} %param.17) | copy-start | bytes 940804
  2.8 1.7 %copy-start.1 = (bf16[280,1680]{1,0:T(8,128)(2,1)S(1)}, bf16[280,1680]{1,0:T(8,128)(2,1)}, u32[]{:S(2)}) copy-start(bf16[280,1680]{1,0:T(8,128)(2,1)} %up_ref.1) | copy-start | bytes 2822404
  2.8 1.7 %copy-start.2 = (bf16[1680,280]{0,1:T(8,128)(2,1)S(1)}, bf16[1680,280]{0,1:T(8,128)(2,1)}, u32[]{:S(2)}) copy-start(bf16[1680,280]{0,1:T(8,128)(2,1)} %param.21) | copy-start | bytes 2822404
  4.5 0.9 copy-start.3
